TPU v7x, 32 devices: a whole 2x2x4 slice. The times are simulated.
32 devices in a mesh: ctx: 8 (over y, x, core), fsdp: 4 (over z).
Axes of the slice: x: 2, y: 2, z: 4, core: 2. Of those that a mesh axis runs over, the one named last changes fastest.
Arguments:
- hidden_in: bfloat16 [4096, 2048], P(('ctx', 'fsdp')), may hold values from -16 to 16
- pair_order: int32 [8], replicated, may hold values from 0 to 7, each once
- attn_gain: bfloat16 [2048], P(('ctx', 'fsdp')), may hold values from 0.099609375 to 1.8984375
- w_query: bfloat16 [2048, 2048], P(('ctx', 'fsdp')), may hold values from -0.21875 to 0.21875
- key_weight_matrix: bfloat16 [2048, 512], P(('ctx', 'fsdp')), may hold values from -0.21875 to 0.21875
- value_weight_matrix: bfloat16 [2048, 512], P(('ctx', 'fsdp')), may hold values from -0.125 to 0.125
- w_out: bfloat16 [2048, 2048], P(('ctx', 'fsdp')), may hold values from -0.125 to 0.125
- mlp_gain: bfloat16 [2048], P(('ctx', 'fsdp')), may hold values from 0.099609375 to 1.8984375
- w_gate: bfloat16 [2048, 8192], P(('ctx', 'fsdp')), may hold values from -0.125 to 0.125
- w_up: bfloat16 [2048, 8192], P(('ctx', 'fsdp')), may hold values from -0.125 to 0.125
- w_down: bfloat16 [8192, 2048], P(None, ('ctx', 'fsdp')), may hold values from -0.0625 to 0.0625
- out_grad: bfloat16 [4096, 2048], P(('ctx', 'fsdp')), may hold values from -6 to 6
Outputs:
- result: float32 [4096, 2048], P(('ctx', 'fsdp'))
- grad_in: float32 [4096, 2048], P(('ctx', 'fsdp'))
- grad_attn_gain: float32 [2048], P(('ctx', 'fsdp'))
- grad_query: float32 [2048, 2048], P(('ctx', 'fsdp'))
- grad_key: float32 [2048, 512], P(('ctx', 'fsdp'))
- grad_value: float32 [2048, 512], P(('ctx', 'fsdp'))
- grad_out: float32 [2048, 2048], P(('ctx', 'fsdp'))
- grad_mlp_gain: float32 [2048], P(('ctx', 'fsdp'))
- grad_gate: float32 [2048, 8192], P(('ctx', 'fsdp'))
- grad_up: float32 [2048, 8192], P(('ctx', 'fsdp'))
- grad_down: float32 [8192, 2048], P(None, ('ctx', 'fsdp'))
Inputs may be any that keep to these rules, and one draw needn't show every extreme that they name: `pair_order`: a permutation of the 8 pairs of causal blocks.
All inputs are finite; a program needn't handle non-finite values.
Results may differ from a plain program's by a relative error of at most 0.017.
The roundings to bfloat16 on the way count: a program that leaves them out, or rounds other values in their place, can miss the bound.
Values may be sent and summed in bfloat16 or wider, within the bound.
No kernel may reach another device: no remote copies, remote signals or barrier semaphores. Data moves between devices by JAX's collectives and lax.ppermute only.
A program may use at most 512 MiB of HBM per device.

v0:
```python
import functools

import jax
import jax.numpy as jnp
from jax import lax
from jax.experimental import pallas as pl
from jax.experimental.pallas import tpu as pltpu
from jax.sharding import PartitionSpec as P


QUERY_HEADS = 32
KEY_VALUE_HEADS = 8
HEAD_SIZE = 64
LANES = 128

rope_base = 500000.0
norm_eps = 1e-05
CTX, FSDP = BOTH = ("ctx", "fsdp")
BF16, F32 = jnp.bfloat16, jnp.float32


NT = (((1,), (1,)), ((), ()))
TN = (((0,), (0,)), ((), ()))
NN = (((1,), (0,)), ((), ()))


def mm(a, b, dims=NN, out=F32):
    return lax.dot_general(a, b, dims, preferred_element_type=F32).astype(out)


def shift_perm(n, s):
    return [(i, (i + s) % n) for i in range(n)]


def z_gather(x):
    n = lax.axis_size(FSDP)
    parts = [x] + [lax.ppermute(x, FSDP, shift_perm(n, s)) for s in range(1, n)]
    return jnp.concatenate(parts, axis=0)


def z_reduce(partial):
    n = lax.axis_size(FSDP)
    rows = partial.shape[0] // n
    total = partial[:rows].astype(F32)
    for s in range(1, n):
        piece = partial[s * rows : (s + 1) * rows].astype(BF16)
        total = total + lax.ppermute(piece, FSDP, shift_perm(n, -s)).astype(F32)
    return total


def z_exchange(x):
    return lax.all_to_all(x, FSDP, 0, 0, tiled=True)


def z_sum(pick):
    n, me = lax.axis_size(FSDP), lax.axis_index(FSDP)
    total = pick(me).astype(F32)
    for s in range(1, n):
        got = lax.ppermute(pick((me + s) % n), FSDP, shift_perm(n, s))
        total = total + got.astype(F32)
    return total


def z_spread(pick):
    n, me = lax.axis_size(FSDP), lax.axis_index(FSDP)
    own = pick(me)
    out = jnp.zeros((n,) + own.shape, own.dtype)
    out = lax.dynamic_update_index_in_dim(out, own, me, 0)
    for s in range(1, n):
        got = lax.ppermute(pick((me + s) % n), FSDP, shift_perm(n, s))
        out = lax.dynamic_update_index_in_dim(out, got, (me - s) % n, 0)
    return out


def ctx_gather(x):
    return lax.all_gather(x, CTX, axis=0, tiled=True)


def ctx_reduce(x):
    return lax.psum_scatter(x, CTX, scatter_dimension=0, tiled=True)


def xor_slots(n):
    return list(range(0, n, 2)) + list(range(1, n, 2))


def xor_swap(x, bit):
    n = lax.axis_size(CTX)
    return lax.ppermute(x, CTX, [(i, i ^ bit) for i in range(n)])


def bit_orders(n):
    bits = [1 << b for b in range(1, n.bit_length() - 1)]
    return bits, bits[::-1]


def xor_gather(x):
    n, rows = lax.axis_size(CTX), x.shape[0] // 2
    halves = []
    for order, piece in zip(bit_orders(n), (x[:rows], x[rows:])):
        parts = {0: piece}
        for bit in order:
            parts.update({m ^ bit: xor_swap(part, bit) for m, part in list(parts.items())})
        halves.append(parts)
    mine = jnp.stack(
        [jnp.concatenate([half[m] for half in halves], axis=0) for m in xor_slots(n)[: n // 2]]
    )
    return jnp.concatenate([mine, xor_swap(mine, 1)], axis=0)


def xor_reduce(x):
    n, rows = lax.axis_size(CTX), x.shape[1] // 2
    got = xor_swap(x[n // 2 :], 1)
    mine = (x[: n // 2].astype(F32) + got.astype(F32)).astype(BF16)
    done = []
    for order, cut in zip(bit_orders(n), (slice(None, rows), slice(rows, None))):
        parts = {m: mine[i, cut] for i, m in enumerate(xor_slots(n)[: n // 2])}
        for bit in order:
            away = sorted(m for m in parts if m & bit)
            got = xor_swap(jnp.stack([parts[m] for m in away]), bit)
            for i, m in enumerate(away):
                kept = parts[m ^ bit].astype(F32) + got[i].astype(F32)
                parts[m ^ bit] = kept if len(away) == 1 else kept.astype(BF16)
                del parts[m]
        done.append(parts[0])
    return jnp.concatenate(done, axis=0)


def after(x, *others):
    return lax.optimization_barrier((x,) + others)[0]


def rotate_tile(x, cosine, sine):
    lane = lax.broadcasted_iota(jnp.int32, x.shape, 1)
    low = (lane % HEAD_SIZE) < HEAD_SIZE // 2
    width = x.shape[1]
    swapped = jnp.where(
        low, pltpu.roll(x, width - HEAD_SIZE // 2, 1), pltpu.roll(x, HEAD_SIZE // 2, 1)
    )
    return x * cosine + swapped * sine


def rotate_tables(positions):
    lane = jnp.arange(LANES, dtype=jnp.int32)
    frequency = 1.0 / rope_base ** (
        jnp.arange(0, HEAD_SIZE, 2, dtype=F32) / HEAD_SIZE
    )
    frequency = jnp.tile(frequency, LANES // (HEAD_SIZE // 2))
    angles = positions.astype(F32)[:, None] * frequency[None, :]
    sign = jnp.where((lane % HEAD_SIZE) < HEAD_SIZE // 2, -1.0, 1.0)
    return jnp.cos(angles), jnp.sin(angles) * sign[None, :]


def project_body(
    x_ref, gain_ref, w_ref, cos_ref, sin_ref, normed_ref, out_ref, flat_ref, *, query_width, rows
):
    @pl.when(pl.program_id(0) == 0)
    def _():
        flat_ref[...] = w_ref[:, :, :rows, :].reshape(flat_ref.shape)

    x = x_ref[...].astype(F32)
    scale = lax.rsqrt(jnp.mean(x * x, axis=1, keepdims=True) + norm_eps)
    normed = (x * scale * gain_ref[...]).astype(BF16)
    normed_ref[...] = normed
    tile = jnp.dot(normed, flat_ref[...], preferred_element_type=F32)
    for i in range(out_ref.shape[1] // LANES):
        part = tile[:, i * LANES : (i + 1) * LANES]
        column = i * LANES + lax.broadcasted_iota(jnp.int32, part.shape, 1)
        turned = rotate_tile(part, cos_ref[...], sin_ref[...])
        part = jnp.where(column < query_width + HEAD_SIZE, turned, part)
        scale = jnp.where(column < query_width, HEAD_SIZE ** (-0.5), 1.0)
        out_ref[:, i * LANES : (i + 1) * LANES] = (part * scale).astype(BF16)


def project(x, gain, w, cosine, sine, query_width, w_rows):
    rows, depth = x.shape
    width = w.shape[3]
    tile = min(rows, 256)
    return pl.pallas_call(
        functools.partial(project_body, query_width=query_width, rows=w_rows),
        out_shape=(
            jax.ShapeDtypeStruct((rows, depth), BF16),
            jax.ShapeDtypeStruct((rows, width), BF16),
            jax.ShapeDtypeStruct((depth, width), BF16),
        ),
        grid=(rows // tile,),
        in_specs=[
            pl.BlockSpec((tile, depth), lambda i: (i, 0)),
            pl.BlockSpec((1, depth), lambda i: (0, 0)),
            pl.BlockSpec(w.shape, lambda i: (0, 0, 0, 0)),
            pl.BlockSpec((tile, LANES), lambda i: (i, 0)),
            pl.BlockSpec((tile, LANES), lambda i: (i, 0)),
        ],
        out_specs=[
            pl.BlockSpec((tile, depth), lambda i: (i, 0)),
            pl.BlockSpec((tile, width), lambda i: (i, 0)),
            pl.BlockSpec((depth, width), lambda i: (0, 0)),
        ],
        name="project",
    )(x, gain, w, cosine, sine)


def unrotate_body(x_ref, cos_ref, sin_ref, out_ref):
    part = x_ref[...]
    lane = lax.broadcasted_iota(jnp.int32, part.shape, 1)
    turned = rotate_tile(part, cos_ref[...], -sin_ref[...])
    out_ref[...] = jnp.where(lane < HEAD_SIZE, turned, part).astype(BF16)


def unrotate(x, cosine, sine):
    return pl.pallas_call(
        unrotate_body, out_shape=jax.ShapeDtypeStruct(x.shape, BF16), name="unrotate"
    )(x, cosine, sine)


def stack_heads(x, heads, high):
    out = []
    for h in range(heads):
        tile = x[:, (h // 2) * LANES : (h // 2 + 1) * LANES].astype(F32)
        if (h % 2 == 1) != high:
            tile = pltpu.roll(tile, HEAD_SIZE, 1)
        lane = lax.broadcasted_iota(jnp.int32, tile.shape, 1)
        out.append(jnp.where((lane >= HEAD_SIZE) == high, tile, 0.0))
    return jnp.concatenate(out, axis=0)


def join_heads(stacked, heads, high):
    rows = stacked.shape[0] // heads
    for pair in range(heads // 2):
        even = stacked[2 * pair * rows : (2 * pair + 1) * rows]
        odd = stacked[(2 * pair + 1) * rows : (2 * pair + 2) * rows]
        if high:
            even = pltpu.roll(even, HEAD_SIZE, 1)
        else:
            odd = pltpu.roll(odd, HEAD_SIZE, 1)
        lane = lax.broadcasted_iota(jnp.int32, even.shape, 1)
        yield slice(pair * LANES, (pair + 1) * LANES), jnp.where(lane < HEAD_SIZE, even, odd)


def lane_sums(e):
    total = e[:, :LANES]
    for i in range(1, e.shape[1] // LANES):
        total = total + e[:, i * LANES : (i + 1) * LANES]
    return total


def across(x):
    return jnp.sum(x.T, axis=0, keepdims=True)


def items(meta, step, n_blocks):
    early = meta[step]
    place = lambda block: meta[n_blocks // 2 + block]
    for half in range(2):
        yield half, place(early if half == 0 else n_blocks - 1 - early), True
    for t in range(n_blocks - 1):
        late = t >= early
        yield late.astype(jnp.int32), place(jnp.where(late, t - early, t)), False


def attend_body(
    meta, q_ref, kv_ref, row_ref, col_ref, o_ref, ob_ref, linv_ref, qs_ref, acc_ref, l_ref, *, heads
):
    step = pl.program_id(0)
    n_slots, n_pairs, _, rows, _ = kv_ref.shape
    for half in range(2):
        qs_ref[half] = stack_heads(q_ref[0, half], heads, False).astype(BF16)
    acc_ref[...] = jnp.zeros_like(acc_ref)
    l_ref[...] = jnp.zeros_like(l_ref)
    for half, place, diagonal in items(meta, step, 2 * n_pairs):
        kv = kv_ref[:, place // 2, place % 2].reshape(n_slots * rows, LANES)
        e = jnp.exp(lax.dot_general(qs_ref[half], kv, NT, preferred_element_type=F32))
        if diagonal:
            e = jnp.where(col_ref[0:1, :] <= row_ref[:, 0:1], e, 0.0)
        l_ref[half] += lane_sums(e)
        acc_ref[half] += jnp.dot(e.astype(BF16), kv, preferred_element_type=F32)
    for half in range(2):
        sums = l_ref[half]
        linv_ref[0, half : half + 1, :] = 1.0 / across(sums)
        out = acc_ref[half] * (1.0 / jnp.sum(sums, axis=1, keepdims=True))
        for columns, tile in join_heads(out, heads, True):
            o_ref[0, half, :, columns] = tile
            ob_ref[0, half, :, columns] = tile.astype(BF16)


def attend_back_body(
    meta, q_ref, do_ref, o_ref, kv_ref, linv_ref, row_ref, col_ref, cos_ref, sin_ref,
    dq_ref, dkv_ref, qd_ref, delta_ref, dq_acc, dkv_acc, *, heads
):
    step = pl.program_id(0)
    n_slots, n_pairs, _, rows, _ = kv_ref.shape
    span, tall = n_slots * rows, heads * rows

    @pl.when(step == 0)
    def _():
        dkv_acc[...] = jnp.zeros_like(dkv_acc)

    dq_acc[...] = jnp.zeros_like(dq_acc)
    for half in range(2):
        qd_ref[half, :tall] = stack_heads(q_ref[0, half], heads, False).astype(BF16)
        do = stack_heads(do_ref[0, half], heads, True)
        qd_ref[half, tall:] = do.astype(BF16)
        delta_ref[half] = across(do * stack_heads(o_ref[0, half], heads, True))
    for half, place, diagonal in items(meta, step, 2 * n_pairs):
        kv = kv_ref[:, place // 2, place % 2].reshape(span, LANES)
        e = jnp.exp(lax.dot_general(kv, qd_ref[half, :tall], NT, preferred_element_type=F32))
        p = e * linv_ref[0, pl.ds(half, 1), :]
        if diagonal:
            p = jnp.where(row_ref[:, 0:1] <= col_ref[0:1, :], p, 0.0)
        dp = lax.dot_general(kv, qd_ref[half, tall:], NT, preferred_element_type=F32)
        ds = (p * (dp - delta_ref[half])).astype(BF16)
        dkv_acc[place] += jnp.dot(
            jnp.concatenate([ds, p.astype(BF16)], axis=1), qd_ref[half], preferred_element_type=F32
        )
        dq_acc[half] += lax.dot_general(ds, kv, TN, preferred_element_type=F32)
    for half in range(2):
        for columns, tile in join_heads(dq_acc[half] * HEAD_SIZE ** (-0.5), heads, False):
            turned = rotate_tile(tile, cos_ref[0, half], -sin_ref[0, half])
            dq_ref[0, half, :, columns] = turned.astype(BF16)

    @pl.when(step == pl.num_programs(0) - 1)
    def _():
        for place in range(2 * n_pairs):
            dkv_ref[:, place // 2, place % 2] = (
                dkv_acc[place].astype(BF16).reshape(n_slots, rows, LANES)
            )


def attention_specs(kv_all):
    _, _, _, rows, _ = kv_all.shape
    pair = lambda w: pl.BlockSpec((1, 2, rows, w), lambda j, m: (j, 0, 0, 0))
    held = lambda x: pl.BlockSpec(x.shape, lambda j, m: (0,) * len(x.shape))
    return pair, held


def attend(meta, qkv, kv_all, row_pos, col_pos, heads):
    _, n_pairs, _, rows, _ = kv_all.shape
    width = heads * HEAD_SIZE
    pair, held = attention_specs(kv_all)
    across_spec = pl.BlockSpec((1, 2, heads * rows), lambda j, m: (j, 0, 0))
    return pl.pallas_call(
        functools.partial(attend_body, heads=heads),
        out_shape=(
            jax.ShapeDtypeStruct((n_pairs, 2, rows, width), F32),
            jax.ShapeDtypeStruct((n_pairs, 2, rows, width), BF16),
            jax.ShapeDtypeStruct((n_pairs, 2, heads * rows), F32),
        ),
        grid_spec=pltpu.PrefetchScalarGridSpec(
            num_scalar_prefetch=1,
            grid=(n_pairs,),
            in_specs=[pair(width), held(kv_all), held(row_pos), held(col_pos)],
            out_specs=[pair(width), pair(width), across_spec],
            scratch_shapes=[
                pltpu.VMEM((2, heads * rows, LANES), BF16),
                pltpu.VMEM((2, heads * rows, LANES), F32),
                pltpu.VMEM((2, heads * rows, LANES), F32),
            ],
        ),
        name="attend",
    )(meta, qkv, kv_all, row_pos, col_pos)


def attend_back(meta, qkv, do, o, kv_all, linv, row_pos, col_pos, cosine, sine, heads):
    n_slots, n_pairs, _, rows, _ = kv_all.shape
    width, tall = heads * HEAD_SIZE, heads * rows
    pair, held = attention_specs(kv_all)
    across_spec = pl.BlockSpec((1, 2, tall), lambda j, m: (j, 0, 0))
    return pl.pallas_call(
        functools.partial(attend_back_body, heads=heads),
        out_shape=(
            jax.ShapeDtypeStruct((n_pairs, 2, rows, width), BF16),
            jax.ShapeDtypeStruct(kv_all.shape, BF16),
        ),
        grid_spec=pltpu.PrefetchScalarGridSpec(
            num_scalar_prefetch=1,
            grid=(n_pairs,),
            in_specs=[
                pair(width), pair(width), pair(width), held(kv_all), across_spec,
                held(row_pos), held(col_pos), pair(LANES), pair(LANES),
            ],
            out_specs=[pair(width), held(kv_all)],
            scratch_shapes=[
                pltpu.VMEM((2, 2 * tall, LANES), BF16),
                pltpu.VMEM((2, 1, tall), F32),
                pltpu.VMEM((2, tall, LANES), F32),
                pltpu.VMEM((2 * n_pairs, n_slots * rows, LANES), F32),
            ],
        ),
        name="attend_back",
    )(meta, qkv, do, o, kv_all, linv, row_pos, col_pos, cosine, sine)


def shards(
    hidden_in,
    pair_order,
    attn_gain,
    w_query,
    key_weight_matrix,
    value_weight_matrix,
    w_out,
    mlp_gain,
    w_gate,
    w_up,
    w_down,
    out_grad,
):
    n_ctx, n_fsdp = lax.axis_size(CTX), lax.axis_size(FSDP)
    my_ctx, my_fsdp = lax.axis_index(CTX), lax.axis_index(FSDP)
    resident_rows, model_width = hidden_in.shape
    half_rows = resident_rows // 2
    span = half_rows * n_fsdp
    plane_rows = resident_rows * n_ctx
    heads = QUERY_HEADS // n_ctx
    sharers = max(1, n_ctx // KEY_VALUE_HEADS)
    query_width = heads * HEAD_SIZE
    qkv_width = query_width + 2 * HEAD_SIZE
    hidden_units = w_gate.shape[1]
    unit_slice = hidden_units // n_fsdp
    weight_rows = w_gate.shape[0]

    labels = jnp.arange(n_ctx, dtype=jnp.int32)
    slot_device = my_ctx ^ jnp.array(xor_slots(n_ctx), jnp.int32)
    slot_pair = jnp.sum(
        jnp.where(slot_device[:, None] == labels[None, :], pair_order[None, :], 0), axis=1
    )
    slot_blocks = jnp.stack([slot_pair, 2 * n_ctx - 1 - slot_pair], axis=1)
    blocks = jnp.arange(2 * n_ctx, dtype=jnp.int32)
    place_of = jnp.sum(
        jnp.where(slot_blocks.reshape(-1)[None, :] == blocks[:, None], blocks[None, :], 0), axis=1
    )
    meta = jnp.concatenate([slot_pair, place_of]).astype(jnp.int32)
    in_half = jnp.arange(half_rows, dtype=jnp.int32)
    my_pos = my_fsdp * half_rows + in_half
    positions = (slot_blocks[:, :, None] * span + my_pos).reshape(plane_rows)
    cosine, sine = rotate_tables(positions)
    slot_owner = (my_fsdp - jnp.arange(n_fsdp, dtype=jnp.int32)) % n_fsdp
    key_pos = (slot_owner[:, None] * half_rows + in_half[None, :]).reshape(span)
    query_pos = jnp.tile(my_pos, heads)
    as_rows = lambda v: jnp.broadcast_to(v[:, None], v.shape + (LANES,))
    as_columns = lambda v: jnp.broadcast_to(v[None, :], (8,) + v.shape)

    padded_rows = weight_rows + 8
    kv_of = lambda w: jnp.repeat(
        w.reshape(weight_rows, -1, HEAD_SIZE).transpose(1, 0, 2), sharers, axis=0
    )
    w_first = jnp.concatenate(
        [
            w_query.reshape(weight_rows, n_ctx, query_width).transpose(1, 0, 2),
            kv_of(key_weight_matrix),
            kv_of(value_weight_matrix),
        ],
        axis=2,
    )
    both_gains = jnp.concatenate([attn_gain, mlp_gain])
    gain_block = jnp.pad(both_gains[None, :], ((0, 7), (0, qkv_width - 2 * weight_rows)))
    w_first = jnp.concatenate(
        [w_first, jnp.broadcast_to(gain_block, (n_ctx,) + gain_block.shape)], axis=1
    )
    w_first = lax.all_to_all(w_first, CTX, 0, 0, tiled=True)
    w_first = lax.all_gather(w_first, FSDP, axis=1, tiled=True)
    w_first = w_first.reshape(n_ctx, n_fsdp, padded_rows, qkv_width)
    all_gains = w_first[:, :, weight_rows, : 2 * weight_rows].astype(F32)
    gain_one = all_gains[:, :, :weight_rows].reshape(1, model_width)
    gain_two = all_gains[:, :, weight_rows:].reshape(1, model_width)

    hidden_all = xor_gather(hidden_in).reshape(plane_rows, model_width)
    normed_one, qkv, w_qkv = project(
        hidden_all, gain_one, w_first, cosine, sine, query_width, weight_rows
    )
    qkv4 = qkv.reshape(n_ctx, 2, half_rows, qkv_width)
    kv_all = z_gather(qkv[:, query_width:])
    kv_all = kv_all.reshape(n_fsdp, n_ctx, 2, half_rows, LANES)


    def by_slice(w):
        return w.reshape(weight_rows, n_fsdp, unit_slice).transpose(1, 0, 2)

    def exchange_two(a, b, *others):
        both = jnp.concatenate([a, b], axis=2)
        both = z_exchange(after(both, *others))
        return both[..., : a.shape[2]], both[..., a.shape[2] :]

    def whole(mine):
        return ctx_gather(mine.reshape(n_fsdp * weight_rows, -1))

    w_out_slice = z_spread(lambda d: w_out).reshape(-1, model_width)
    gate_mine = z_spread(lambda d: lax.dynamic_slice_in_dim(w_gate, d * unit_slice, unit_slice, 1))
    gate_w = whole(gate_mine)
    up_mine, down_mine = exchange_two(by_slice(w_up), by_slice(w_down.T), kv_all)
    up_w, down_t = whole(up_mine), whole(down_mine)
    grad_all = z_gather(after(out_grad, up_mine))

    o_full, o_b, linv = attend(
        meta, qkv4, after(kv_all, gate_mine), as_rows(query_pos), as_columns(key_pos), heads
    )
    o_b = o_b.reshape(plane_rows, query_width)
    residual = hidden_in.astype(F32)
    out_product = mm(o_b, w_out_slice, NN, BF16)
    attn_out = xor_reduce(out_product.reshape(n_ctx, resident_rows, -1))
    after_attn = residual + attn_out
    scale_two = lax.rsqrt(jnp.mean(after_attn * after_attn, axis=1, keepdims=True) + norm_eps)
    unit_two = after_attn * scale_two
    normed_two = z_gather((unit_two * gain_two).astype(BF16))

    gate_proj = mm(normed_two, gate_w)
    up_proj = mm(normed_two, up_w)
    gate_proj, up_proj = lax.optimization_barrier((gate_proj, up_proj))
    d_act = mm(grad_all, down_t)
    sigmoid_gate = jax.nn.sigmoid(gate_proj)
    activated = (gate_proj * sigmoid_gate * up_proj).astype(BF16)
    d_gate = (d_act * up_proj * sigmoid_gate * (1.0 + gate_proj * (1.0 - sigmoid_gate))).astype(
        BF16
    )
    d_up = (d_act * gate_proj * sigmoid_gate).astype(BF16)
    d_normed_partial = (mm(d_gate, gate_w, NT) + mm(d_up, up_w, NT)).astype(BF16)
    d_normed_two = z_reduce(d_normed_partial)

    ffn_partials = [
        mm(after(grad_all, d_normed_partial), activated, TN, BF16),
        mm(after(normed_two, d_normed_partial), d_gate, TN, BF16),
        mm(after(normed_two, d_normed_partial), d_up, TN, BF16),
    ]
    ffn_grads = [ctx_reduce(g) for g in ffn_partials]
    result_partial = mm(after(activated, d_normed_two), down_t, NT, BF16)
    result = after_attn + z_reduce(after(result_partial, d_normed_two))

    gain_two_grad = jnp.sum(d_normed_two * unit_two, axis=0)
    d_unit_two = d_normed_two * gain_two
    d_mixed = out_grad.astype(F32) + scale_two * (
        d_unit_two - unit_two * jnp.mean(d_unit_two * unit_two, axis=1, keepdims=True)
    )
    d_attn = xor_gather(d_mixed.astype(BF16)).reshape(plane_rows, model_width)
    d_attn = after(d_attn, *ffn_partials)
    d_o = mm(d_attn, w_out_slice, NT, BF16)
    out_partial = mm(o_b, d_attn, TN, BF16).reshape(n_fsdp, weight_rows, model_width)
    grad_out_w = z_sum(lambda d: lax.dynamic_index_in_dim(out_partial, d, 0, False))
    pair_view = lambda x: x.reshape(n_ctx, 2, half_rows, -1)
    dq, dkv_all = attend_back(
        meta,
        qkv4,
        pair_view(d_o),
        o_full,
        kv_all,
        linv,
        as_rows(key_pos),
        as_columns(query_pos),
        pair_view(cosine),
        pair_view(sine),
        heads,
    )
    dkv = z_reduce(dkv_all.reshape(n_fsdp * plane_rows, LANES))
    dkv = unrotate(dkv, cosine, sine)
    d_qkv = jnp.concatenate([dq.reshape(plane_rows, query_width), dkv], axis=1)
    d_first_partial = mm(d_qkv, w_qkv, NT, BF16)
    d_normed_one = xor_reduce(d_first_partial.reshape(n_ctx, resident_rows, -1))

    scale_one = lax.rsqrt(jnp.mean(residual * residual, axis=1, keepdims=True) + norm_eps)
    unit_one = residual * scale_one
    d_unit_one = d_normed_one * gain_one
    grad_in = d_mixed + scale_one * (
        d_unit_one - unit_one * jnp.mean(d_unit_one * unit_one, axis=1, keepdims=True)
    )

    wide = hidden_all.astype(F32)
    scale_all = lax.rsqrt(jnp.mean(wide * wide, axis=1, keepdims=True) + norm_eps)
    gain_one_grad = jnp.sum(d_first_partial.astype(F32) * (wide * scale_all), axis=0)
    by_owner = lambda g: g.reshape(n_ctx, n_fsdp, weight_rows)
    gain_grads = jnp.concatenate([by_owner(gain_one_grad), by_owner(gain_two_grad)], axis=2)
    gain_grads = jnp.pad(
        gain_grads[:, :, None, :].astype(BF16),
        ((0, 0), (0, 0), (0, 7), (0, qkv_width - 2 * weight_rows)),
    )
    first_grads = mm(normed_one, d_qkv, TN, BF16).reshape(n_ctx, n_fsdp, weight_rows, qkv_width)
    first_grads = jnp.concatenate(
        [first_grads.transpose(1, 0, 2, 3), gain_grads.transpose(1, 0, 2, 3)], axis=2
    )
    first_sum = jnp.sum(z_exchange(first_grads).astype(F32), axis=0)
    first_home = lax.all_to_all(first_sum.astype(BF16), CTX, 0, 0, tiled=True).astype(F32)

    def part_home(start, width, share):
        part = first_home[:, :weight_rows, start : start + width]
        part = jnp.sum(part.reshape(n_ctx // share, share, weight_rows, width), axis=1)
        return part.transpose(1, 0, 2).reshape(weight_rows, -1)

    query_sum = part_home(0, query_width, 1)
    key_sum = part_home(query_width, HEAD_SIZE, sharers)
    value_sum = part_home(query_width + HEAD_SIZE, HEAD_SIZE, sharers)
    gain_sums = jnp.sum(first_home[:, weight_rows, : 2 * weight_rows], axis=0)

    def columns_home(pieces):
        return pieces.transpose(1, 0, 2).reshape(weight_rows, hidden_units).astype(F32)

    homes = [g.reshape(n_fsdp, weight_rows, unit_slice) for g in ffn_grads]
    down_sum = columns_home(z_exchange(homes[0]))
    gate_sum = columns_home(z_exchange(homes[1]))
    up_pick = lambda d: lax.dynamic_index_in_dim(homes[2], d, 0, False)
    up_sum = columns_home(z_spread(up_pick))
    return (
        result,
        grad_in,
        gain_sums[:weight_rows],
        query_sum,
        key_sum,
        value_sum,
        grad_out_w,
        gain_sums[weight_rows:],
        gate_sum,
        up_sum,
        down_sum.T,
    )


def solution(mesh):
    rows, columns, vector = P(BOTH, None), P(None, BOTH), P(BOTH)
    placed = (rows, P(), vector, rows, rows, rows, rows, vector, rows, rows, columns, rows)

    return jax.shard_map(
        shards,
        mesh=mesh,
        in_specs=placed,
        out_specs=(rows, rows, vector, rows, rows, rows, rows, vector, rows, rows, columns),
        check_vma=False,
    )
```

profile of v0, /device:TPU:0, one launch (start us, length us, event | category | flops | bytes accessed | tf_op | source)
XLA Modules:
  0.0 855.3 jit_solution(3371590122509740779)
XLA Ops:
  11.2 13.9 %all_to_all.30 = bf16[8,72,384]{2,1,0:T(8,128)(2,1)} all-to-all(bf16[8,72,384]{2,1,0:T(8,128)(2,1)S(1)} %pad_maximum_fusion.11), channel_id=1, replica_groups=mesh['ctx'=8,'fsdp'=4] {'ctx'}, dimensions={0} | all-to-all | bytes 884736 | tf_op jit(solution)/shard_map/all_to_all | solution.py:459
  31.1 5.5 collective-permute-done.10
  37.6 20.5 %collective-permute-done.11 = bf16[64,2048]{1,0:T(8,128)(2,1)} collective-permute-done((bf16[64,2048]{1,0:T(8,128)(2,1)S(1)}, bf16[64,2048]{1,0:T(8,128)(2,1)}, u32[]{:S(2)}, u32[]{:S(2)}) %collective-permute-start.11) | collective-permute-done | bytes 262176 | tf_op jit(solution)/shard_map/ppermute | solution.py:70
  65.4 5.8 collective-permute-done.3
  98.4 7.7 project.1
  107.1 12.0 %collective-permute-start.9 = (bf16[1024,128]{1,0:T(8,128)(2,1)S(1)}, bf16[1024,128]{1,0:T(8,128)(2,1)S(1)}, u32[]{:S(2)}, u32[]{:S(2)}) collective-permute-start(bf16[1024,128]{1,0:T(8,128)(2,1)S(1)} %slice.186), channel_id=1, source_target_pairs={{0,3},{1,0},{2,1},{3,2},{4,7},{5,4},{6,5},{7,6},{8,11},{9,8},{10,9... | collective-permute-start | bytes 786440 | tf_op jit(solution)/shard_map/ppermute | solution.py:37
  119.1 13.4 %collective-permute-start.8 = (bf16[1024,128]{1,0:T(8,128)(2,1)S(1)}, bf16[1024,128]{1,0:T(8,128)(2,1)S(1)}, u32[]{:S(2)}, u32[]{:S(2)}) collective-permute-start(bf16[1024,128]{1,0:T(8,128)(2,1)S(1)} %slice.186), channel_id=1, source_target_pairs={{0,2},{1,3},{2,0},{3,1},{4,6},{5,7},{6,4},{7,5},{8,10},{9,11},{10,... | collective-permute-start | bytes 786440 | tf_op jit(solution)/shard_map/ppermute | solution.py:37
  138.2 18.0 %collective-permute-done.8 = bf16[1024,128]{1,0:T(8,128)(2,1)S(1)} collective-permute-done((bf16[1024,128]{1,0:T(8,128)(2,1)S(1)}, bf16[1024,128]{1,0:T(8,128)(2,1)S(1)}, u32[]{:S(2)}, u32[]{:S(2)}) %collective-permute-start.8) | collective-permute-done | bytes 262176 | tf_op jit(solution)/shard_map/ppermute | solution.py:37
  158.4 50.9 %all_to_all.31 = bf16[4,64,4096]{2,1,0:T(8,128)(2,1)S(1)} all-to-all(bf16[4,64,4096]{2,1,0:T(8,128)(2,1)S(1)} %copy.90), channel_id=1, replica_groups=mesh['ctx'=8,'fsdp'=4] {'fsdp'}, dimensions={0} | all-to-all | bytes 4194304 | tf_op jit(solution)/shard_map/all_to_all | solution.py:52
  216.3 5.7 collective-permute-done.13
  222.0 9.4 %collective-permute-done.14 = bf16[64,2048]{1,0:T(8,128)(2,1)S(1)} collective-permute-done((bf16[64,2048]{1,0:T(8,128)(2,1)S(1)}, bf16[64,2048]{1,0:T(8,128)(2,1)S(1)}, u32[]{:S(2)}, u32[]{:S(2)}) %collective-permute-start.14) | collective-permute-done | bytes 262176 | tf_op jit(solution)/shard_map/ppermute | solution.py:70
  233.0 16.9 %attend.1 = (f32[8,2,64,256]{3,2,1,0:T(8,128)}, bf16[8,2,64,256]{3,2,1,0:T(8,128)(2,1)}, f32[8,2,256]{2,1,0:T(2,128)}) custom-call(s32[24]{0:T(128)} %pad_add_fusion.1.meta, bf16[8,2,64,384]{3,2,1,0:T(8,128)(2,1)} %bitcast.182, bf16[4,8,2,64,128]{4,3,2,1,0:T(8,128)(2,1)} %bitcast.176, s32[256,128]{1,0:T(8,128)} %broadcast_in_dim.125.row_ref, ...), custom_call_target="tpu_custom_call" | custom-call | tf_op jit(solution)/shard_map/attend/pallas_call | solution.py:341
  253.0 4.7 collective-permute-done.16
  259.0 13.7 %collective-permute-done.17 = bf16[2,64,2048]{2,1,0:T(8,128)(2,1)S(1)} collective-permute-done((bf16[2,64,2048]{2,1,0:T(8,128)(2,1)S(1)}, bf16[2,64,2048]{2,1,0:T(8,128)(2,1)S(1)}, u32[]{:S(2)}, u32[]{:S(2)}) %collective-permute-start.17) | collective-permute-done | bytes 524320 | tf_op jit(solution)/shard_map/ppermute | solution.py:89
  273.3 12.7 %collective-permute-done.18 = bf16[1,64,2048]{2,1,0:T(8,128)(2,1)S(1)} collective-permute-done((bf16[1,64,2048]{2,1,0:T(8,128)(2,1)S(1)}, bf16[1,64,2048]{2,1,0:T(8,128)(2,1)S(1)}, u32[]{:S(2)}, u32[]{:S(2)}) %collective-permute-start.18) | collective-permute-done | bytes 262176 | tf_op jit(solution)/shard_map/ppermute | solution.py:89
  287.0 6.5 collective-permute-done.20
  295.0 6.0 collective-permute-start.23
  308.3 6.2 collective-permute-done.23
  317.9 54.3 %collective-permute-done.22 = bf16[128,2048]{1,0:T(8,128)(2,1)S(1)} collective-permute-done((bf16[128,2048]{1,0:T(8,128)(2,1)S(1)}, bf16[128,2048]{1,0:T(8,128)(2,1)S(1)}, u32[]{:S(2)}, u32[]{:S(2)}) %collective-permute-start.22) | collective-permute-done | bytes 524320 | tf_op jit(solution)/shard_map/ppermute | solution.py:37
  374.6 8.7 %collective-permute-done.25 = bf16[128,2048]{1,0:T(8,128)(2,1)S(1)} collective-permute-done((bf16[128,2048]{1,0:T(8,128)(2,1)S(1)}, bf16[128,2048]{1,0:T(8,128)(2,1)S(1)}, u32[]{:S(2)}, u32[]{:S(2)}) %collective-permute-start.25) | collective-permute-done | bytes 524320 | tf_op jit(solution)/shard_map/ppermute | solution.py:37
  385.1 10.3 %fusion.28 = f32[512,2048]{1,0:T(8,128)} fusion(bf16[2048,2048]{1,0:T(8,128)(2,1)} %all-gather.7.cloned.1.call-done, bf16[128,2048]{1,0:T(8,128)(2,1)S(1)} %collective-permute-done.23, bf16[128,2048]{1,0:T(8,128)(2,1)} %copy-done.32, bf16[128,2048]{1,0:T(8,128)(2,1)} %copy-done.33, bf16[128,2048]{1,0:T(8,128)(2,1)S(1)} %multiply_convert_fusion.3), kind=kOutput, calls=%fused_computation.164 | convolution fusion | flops 4303355904 | bytes 14680064 | tf_op jit(solution)/shard_map/dot_general | solution.py:28
  395.4 10.2 %fusion.27 = f32[512,2048]{1,0:T(8,128)} fusion(bf16[2048,2048]{1,0:T(8,128)(2,1)} %all-gather.9.cloned.1.call-done, bf16[128,2048]{1,0:T(8,128)(2,1)S(1)} %collective-permute-done.23, bf16[128,2048]{1,0:T(8,128)(2,1)} %copy-done.32, bf16[128,2048]{1,0:T(8,128)(2,1)} %copy-done.33, bf16[128,2048]{1,0:T(8,128)(2,1)S(1)} %multiply_convert_fusion.3), kind=kOutput, calls=%fused_computation.163 | convolution fusion | flops 4303355904 | bytes 14680064 | tf_op jit(solution)/shard_map/dot_general | solution.py:28
  405.5 8.2 fusion.42
  417.8 10.3 %fusion.43 = f32[512,2048]{1,0:T(8,128)} fusion(bf16[512,2048]{1,0:T(8,128)(2,1)S(1)} %get-tuple-element.56, bf16[2048,2048]{1,0:T(8,128)(2,1)} %all-gather.9.cloned.1.call-done), kind=kOutput, calls=%fused_computation.178 | convolution fusion | flops 4294967296 | bytes 14680064 | tf_op jit(solution)/shard_map/dot_general | solution.py:28
  428.1 7.5 add_convert_fusion
  435.6 6.9 convolution_convert_fusion.1
  442.8 10.1 %convolution_convert_fusion = bf16[2048,2048]{1,0:T(8,128)(2,1)} fusion(bf16[512,2048]{1,0:T(8,128)(2,1)} %pad_maximum_fusion.1, bf16[512,2048]{1,0:T(8,128)(2,1)} %copy-done.14), kind=kOutput, calls=%fused_computation.2 | convolution fusion | flops 4299161600 | bytes 12582912 | tf_op jit(solution)/shard_map/dot_general | solution.py:28
  454.7 7.9 collective-permute-start.29
  466.3 12.4 %collective-permute-done.29 = bf16[128,2048]{1,0:T(8,128)(2,1)S(1)} collective-permute-done((bf16[128,2048]{1,0:T(8,128)(2,1)S(1)}, bf16[128,2048]{1,0:T(8,128)(2,1)S(1)}, u32[]{:S(2)}, u32[]{:S(2)}) %collective-permute-start.29) | collective-permute-done | bytes 524320 | tf_op jit(solution)/shard_map/ppermute | solution.py:47
  478.6 21.7 %collective-permute-done.28 = bf16[128,2048]{1,0:T(8,128)(2,1)S(1)} collective-permute-done((bf16[128,2048]{1,0:T(8,128)(2,1)S(1)}, bf16[128,2048]{1,0:T(8,128)(2,1)S(1)}, u32[]{:S(2)}, u32[]{:S(2)}) %collective-permute-start.28) | collective-permute-done | bytes 524320 | tf_op jit(solution)/shard_map/ppermute | solution.py:47
  512.0 7.7 collective-permute-done.36
  521.9 7.8 collective-permute-done.35
  538.1 8.8 %convolution_convert_fusion.2 = bf16[2048,2048]{1,0:T(8,128)(2,1)} fusion(bf16[512,2048]{1,0:T(8,128)(2,1)} %constant_dynamic-update-slice_fusion.5, bf16[512,2048]{1,0:T(8,128)(2,1)S(1)} %copy-done.12), kind=kOutput, calls=%fused_computation.4 | convolution fusion | flops 4299161600 | bytes 12582912 | tf_op jit(solution)/shard_map/dot_general | solution.py:28
  558.2 48.3 %attend_back.1 = (bf16[8,2,64,256]{3,2,1,0:T(8,128)(2,1)}, bf16[4,8,2,64,128]{4,3,2,1,0:T(8,128)(2,1)}) custom-call(s32[24]{0:T(128)} %pad_add_fusion.1.meta, bf16[8,2,64,384]{3,2,1,0:T(8,128)(2,1)} %bitcast.183, bf16[8,2,64,256]{3,2,1,0:T(8,128)(2,1)} %bitcast.207, f32[8,2,64,256]{3,2,1,0:T(8,128)} %get-tuple-element.41.o_ref, ...), custom_call_target="tpu_custom_call" | custom-call | tf_op jit(solution)/shard_map/attend_back/pallas_call | solution.py:368
  614.0 6.0 collective-permute-done.42
  620.0 9.9 %collective-permute-done.41 = bf16[1024,128]{1,0:T(8,128)(2,1)} collective-permute-done((bf16[1024,128]{1,0:T(8,128)(2,1)}, bf16[1024,128]{1,0:T(8,128)(2,1)}, u32[]{:S(2)}, u32[]{:S(2)}) %collective-permute-start.41) | collective-permute-done | bytes 262176 | tf_op jit(solution)/shard_map/ppermute | solution.py:47
  634.5 5.3 multiply_reduce_fusion
  642.4 8.4 convolution_convert_fusion.5
  653.2 5.9 collective-permute-start.32
  682.0 5.9 collective-permute-done.44
  689.4 16.0 %collective-permute-done.50 = bf16[64,2048]{1,0:T(8,128)(2,1)S(1)} collective-permute-done((bf16[64,2048]{1,0:T(8,128)(2,1)S(1)}, bf16[64,2048]{1,0:T(8,128)(2,1)S(1)}, u32[]{:S(2)}, u32[]{:S(2)}) %collective-permute-start.50) | collective-permute-done | bytes 262176 | tf_op jit(solution)/shard_map/ppermute | solution.py:59
  705.5 23.6 %collective-permute-start.31 = (bf16[128,2048]{1,0:T(8,128)(2,1)}, bf16[128,2048]{1,0:T(8,128)(2,1)}, u32[]{:S(2)}, u32[]{:S(2)}) collective-permute-start(bf16[128,2048]{1,0:T(8,128)(2,1)} %get-tuple-element.67), channel_id=1, source_target_pairs={{0,2},{1,3},{2,0},{3,1},{4,6},{5,7},{6,4},{7,5},{8,10},{9,11},{10,... | collective-permute-start | bytes 1572872 | tf_op jit(solution)/shard_map/ppermute | solution.py:47
  729.0 17.3 %collective-permute-done.49 = bf16[64,2048]{1,0:T(8,128)(2,1)S(1)} collective-permute-done((bf16[64,2048]{1,0:T(8,128)(2,1)S(1)}, bf16[64,2048]{1,0:T(8,128)(2,1)S(1)}, u32[]{:S(2)}, u32[]{:S(2)}) %collective-permute-start.49) | collective-permute-done | bytes 262176 | tf_op jit(solution)/shard_map/ppermute | solution.py:59
  760.1 5.1 all-to-all-done.3
  792.0 13.7 %collective-permute-done.51 = bf16[64,2048]{1,0:T(8,128)(2,1)S(1)} collective-permute-done((bf16[64,2048]{1,0:T(8,128)(2,1)S(1)}, bf16[64,2048]{1,0:T(8,128)(2,1)S(1)}, u32[]{:S(2)}, u32[]{:S(2)}) %collective-permute-start.51) | collective-permute-done | bytes 262176 | tf_op jit(solution)/shard_map/ppermute | solution.py:70
  806.5 7.2 all-to-all-done.4
  813.6 9.9 %all-to-all-start.5 = ((bf16[4,64,2048]{2,1,0:T(8,128)(2,1)}), bf16[4,64,2048]{2,1,0:T(8,128)(2,1)S(1)}, u32[]{:S(2)}, u32[]{:S(2)}) async-start(bf16[4,64,2048]{2,1,0:T(8,128)(2,1)} %bitcast.203), calls=%async_computation.8 | async-start | bytes 2097152 | tf_op jit(solution)/shard_map/all_to_all | solution.py:52
  830.8 15.4 %all-to-all-done.5 = bf16[4,64,2048]{2,1,0:T(8,128)(2,1)S(1)} async-done(((bf16[4,64,2048]{2,1,0:T(8,128)(2,1)}), bf16[4,64,2048]{2,1,0:T(8,128)(2,1)S(1)}, u32[]{:S(2)}, u32[]{:S(2)}) %all-to-all-start.5) | async-done | bytes 1048608 | tf_op jit(solution)/shard_map/all_to_all | solution.py:52
  (341 shorter events, 219.3 us)
Async XLA Ops:
  7.2 89.6 %all-gather.5.cloned.1.call-start = ((), (), s32[]{:S(2)}) async-start(), calls=%async_computation.9 | async-start | bytes 2211840 | tf_op jit(solution)/shard_map/all_gather | solution.py:460
  25.2 359.9 %all-gather.7.cloned.1.call-start = ((), (), s32[]{:S(2)}) async-start(), calls=%async_computation.10 | async-start | bytes 9437184 | tf_op jit(solution)/shard_map/all_gather | solution.py:76
  27.0 31.1 %collective-permute-start.11 = (bf16[64,2048]{1,0:T(8,128)(2,1)S(1)}, bf16[64,2048]{1,0:T(8,128)(2,1)}, u32[]{:S(2)}, u32[]{:S(2)}) collective-permute-start(bf16[64,2048]{1,0:T(8,128)(2,1)S(1)} %get-tuple-element.92), channel_id=1, source_target_pairs={{0,2},{1,3},{2,0},{3,1},{4,6},{5,7},{6,4},{7,5},{8,10},{9,11},{10,... | collective-permute-start | bytes 786440 | tf_op jit(solution)/shard_map/ppermute | solution.py:70
  29.6 29.5 %collective-permute-start.12 = (bf16[64,2048]{1,0:T(8,128)(2,1)S(1)}, bf16[64,2048]{1,0:T(8,128)(2,1)}, u32[]{:S(2)}, u32[]{:S(2)}) collective-permute-start(bf16[64,2048]{1,0:T(8,128)(2,1)S(1)} %get-tuple-element.90), channel_id=1, source_target_pairs={{0,3},{1,0},{2,1},{3,2},{4,7},{5,4},{6,5},{7,6},{8,11},{9,8},{10,9... | collective-permute-start | bytes 786440 | tf_op jit(solution)/shard_map/ppermute | solution.py:70
  61.0 334.4 %all-gather.9.cloned.1.call-start = ((), (), s32[]{:S(2)}) async-start(), calls=%async_computation.11 | async-start | bytes 9437184 | tf_op jit(solution)/shard_map/all_gather | solution.py:76
  61.1 15.5 %collective-permute-start.1 = (bf16[64,2048]{1,0:T(8,128)(2,1)S(1)}, bf16[64,2048]{1,0:T(8,128)(2,1)S(1)}, u32[]{:S(2)}, u32[]{:S(2)}) collective-permute-start(bf16[64,2048]{1,0:T(8,128)(2,1)S(1)} %get-tuple-element.99), channel_id=1, source_target_pairs={{0,8},{4,12},{8,0},{12,4},{16,24},{20,28},{24,16},{28,20},{1,9},{5... | collective-permute-start | bytes 786440 | tf_op jit(solution)/shard_map/ppermute | solution.py:89
  107.1 31.1 %collective-permute-start.9 = (bf16[1024,128]{1,0:T(8,128)(2,1)S(1)}, bf16[1024,128]{1,0:T(8,128)(2,1)S(1)}, u32[]{:S(2)}, u32[]{:S(2)}) collective-permute-start(bf16[1024,128]{1,0:T(8,128)(2,1)S(1)} %slice.186), channel_id=1, source_target_pairs={{0,3},{1,0},{2,1},{3,2},{4,7},{5,4},{6,5},{7,6},{8,11},{9,8},{10,9... | collective-permute-start | bytes 786440 | tf_op jit(solution)/shard_map/ppermute | solution.py:37
  119.1 37.1 %collective-permute-start.8 = (bf16[1024,128]{1,0:T(8,128)(2,1)S(1)}, bf16[1024,128]{1,0:T(8,128)(2,1)S(1)}, u32[]{:S(2)}, u32[]{:S(2)}) collective-permute-start(bf16[1024,128]{1,0:T(8,128)(2,1)S(1)} %slice.186), channel_id=1, source_target_pairs={{0,2},{1,3},{2,0},{3,1},{4,6},{5,7},{6,4},{7,5},{8,10},{9,11},{10,... | collective-permute-start | bytes 786440 | tf_op jit(solution)/shard_map/ppermute | solution.py:37
  132.5 23.7 %collective-permute-start.7 = (bf16[1024,128]{1,0:T(8,128)(2,1)S(1)}, bf16[1024,128]{1,0:T(8,128)(2,1)S(1)}, u32[]{:S(2)}, u32[]{:S(2)}) collective-permute-start(bf16[1024,128]{1,0:T(8,128)(2,1)S(1)} %slice.186), channel_id=1, source_target_pairs={{0,1},{1,2},{2,3},{3,0},{4,5},{5,6},{6,7},{7,4},{8,9},{9,10},{10,1... | collective-permute-start | bytes 786440 | tf_op jit(solution)/shard_map/ppermute | solution.py:37
  210.8 194.7 %all-gather.11.cloned.1.call-start = ((), (), s32[]{:S(2)}) async-start(), calls=%async_computation.12 | async-start | bytes 9437184 | tf_op jit(solution)/shard_map/all_gather | solution.py:76
  211.2 20.3 %collective-permute-start.14 = (bf16[64,2048]{1,0:T(8,128)(2,1)S(1)}, bf16[64,2048]{1,0:T(8,128)(2,1)S(1)}, u32[]{:S(2)}, u32[]{:S(2)}) collective-permute-start(bf16[64,2048]{1,0:T(8,128)(2,1)S(1)} %copy-done.35), channel_id=1, source_target_pairs={{0,2},{1,3},{2,0},{3,1},{4,6},{5,7},{6,4},{7,5},{8,10},{9,11},{10,... | collective-permute-start | bytes 786440 | tf_op jit(solution)/shard_map/ppermute | solution.py:70
  213.0 18.5 %collective-permute-start.15 = (bf16[64,2048]{1,0:T(8,128)(2,1)S(1)}, bf16[64,2048]{1,0:T(8,128)(2,1)S(1)}, u32[]{:S(2)}, u32[]{:S(2)}) collective-permute-start(bf16[64,2048]{1,0:T(8,128)(2,1)S(1)} %copy-done.35), channel_id=1, source_target_pairs={{0,3},{1,0},{2,1},{3,2},{4,7},{5,4},{6,5},{7,6},{8,11},{9,8},{10,9... | collective-permute-start | bytes 786440 | tf_op jit(solution)/shard_map/ppermute | solution.py:70
  214.8 558.7 %reduce-scatter.4.cloned.1.call-start = ((), (), s32[]{:S(2)}) async-start(), calls=%async_computation.13 | async-start | bytes 9437184 | tf_op jit(solution)/shard_map/reduce_scatter | solution.py:80
  258.8 14.6 %collective-permute-start.19 = (bf16[2,64,2048]{2,1,0:T(8,128)(2,1)S(1)}, bf16[2,64,2048]{2,1,0:T(8,128)(2,1)S(1)}, u32[]{:S(2)}, u32[]{:S(2)}) collective-permute-start(bf16[2,64,2048]{2,1,0:T(8,128)(2,1)S(1)} %stack.69), channel_id=1, source_target_pairs={{0,16},{4,20},{8,24},{12,28},{16,0},{20,4},{24,8},{28,12},{1,17},{... | collective-permute-start | bytes 1572872 | tf_op jit(solution)/shard_map/ppermute | solution.py:89
  295.0 19.5 %collective-permute-start.23 = (bf16[128,2048]{1,0:T(8,128)(2,1)S(1)}, bf16[128,2048]{1,0:T(8,128)(2,1)S(1)}, u32[]{:S(2)}, u32[]{:S(2)}) collective-permute-start(bf16[128,2048]{1,0:T(8,128)(2,1)S(1)} %multiply_convert_fusion.3), channel_id=1, source_target_pairs={{0,3},{1,0},{2,1},{3,2},{4,7},{5,4},{6,5},{7,6},{8,11},{9,8},{10,9... | collective-permute-start | bytes 1572872 | tf_op jit(solution)/shard_map/ppermute | solution.py:37
  301.0 71.2 %collective-permute-start.22 = (bf16[128,2048]{1,0:T(8,128)(2,1)S(1)}, bf16[128,2048]{1,0:T(8,128)(2,1)S(1)}, u32[]{:S(2)}, u32[]{:S(2)}) collective-permute-start(bf16[128,2048]{1,0:T(8,128)(2,1)S(1)} %multiply_convert_fusion.3), channel_id=1, source_target_pairs={{0,2},{1,3},{2,0},{3,1},{4,6},{5,7},{6,4},{7,5},{8,10},{9,11},{10,... | collective-permute-start | bytes 1572872 | tf_op jit(solution)/shard_map/ppermute | solution.py:37
  303.1 69.1 %collective-permute-start.21 = (bf16[128,2048]{1,0:T(8,128)(2,1)S(1)}, bf16[128,2048]{1,0:T(8,128)(2,1)S(1)}, u32[]{:S(2)}, u32[]{:S(2)}) collective-permute-start(bf16[128,2048]{1,0:T(8,128)(2,1)S(1)} %multiply_convert_fusion.3), channel_id=1, source_target_pairs={{0,1},{1,2},{2,3},{3,0},{4,5},{5,6},{6,7},{7,4},{8,9},{9,10},{10,1... | collective-permute-start | bytes 1572872 | tf_op jit(solution)/shard_map/ppermute | solution.py:37
  303.2 70.6 %collective-permute-start.24 = (bf16[128,2048]{1,0:T(8,128)(2,1)S(1)}, bf16[128,2048]{1,0:T(8,128)(2,1)S(1)}, u32[]{:S(2)}, u32[]{:S(2)}) collective-permute-start(bf16[128,2048]{1,0:T(8,128)(2,1)S(1)} %copy-done.2), channel_id=1, source_target_pairs={{0,1},{1,2},{2,3},{3,0},{4,5},{5,6},{6,7},{7,4},{8,9},{9,10},{10,1... | collective-permute-start | bytes 1572872 | tf_op jit(solution)/shard_map/ppermute | solution.py:37
  304.5 78.8 %collective-permute-start.25 = (bf16[128,2048]{1,0:T(8,128)(2,1)S(1)}, bf16[128,2048]{1,0:T(8,128)(2,1)S(1)}, u32[]{:S(2)}, u32[]{:S(2)}) collective-permute-start(bf16[128,2048]{1,0:T(8,128)(2,1)S(1)} %copy-done.2), channel_id=1, source_target_pairs={{0,2},{1,3},{2,0},{3,1},{4,6},{5,7},{6,4},{7,5},{8,10},{9,11},{10,... | collective-permute-start | bytes 1572872 | tf_op jit(solution)/shard_map/ppermute | solution.py:37
  314.5 69.7 %collective-permute-start.26 = (bf16[128,2048]{1,0:T(8,128)(2,1)S(1)}, bf16[128,2048]{1,0:T(8,128)(2,1)S(1)}, u32[]{:S(2)}, u32[]{:S(2)}) collective-permute-start(bf16[128,2048]{1,0:T(8,128)(2,1)S(1)} %copy-done.2), channel_id=1, source_target_pairs={{0,3},{1,0},{2,1},{3,2},{4,7},{5,4},{6,5},{7,6},{8,11},{9,8},{10,9... | collective-permute-start | bytes 1572872 | tf_op jit(solution)/shard_map/ppermute | solution.py:37
  442.6 336.6 %reduce-scatter.6.cloned.1.call-start = ((), (), s32[]{:S(2)}) async-start(), calls=%async_computation.14 | async-start | bytes 9437184 | tf_op jit(solution)/shard_map/reduce_scatter | solution.py:80
  453.0 353.5 %reduce-scatter.8.cloned.1.call-start = ((), (), s32[]{:S(2)}) async-start(), calls=%async_computation.15 | async-start | bytes 9437184 | tf_op jit(solution)/shard_map/reduce_scatter | solution.py:80
  454.7 23.9 %collective-permute-start.29 = (bf16[128,2048]{1,0:T(8,128)(2,1)S(1)}, bf16[128,2048]{1,0:T(8,128)(2,1)S(1)}, u32[]{:S(2)}, u32[]{:S(2)}) collective-permute-start(bf16[128,2048]{1,0:T(8,128)(2,1)S(1)} %get-tuple-element.69), channel_id=1, source_target_pairs={{0,1},{1,2},{2,3},{3,0},{4,5},{5,6},{6,7},{7,4},{8,9},{9,10},{10,1... | collective-permute-start | bytes 1572872 | tf_op jit(solution)/shard_map/ppermute | solution.py:47
  462.6 37.8 %collective-permute-start.28 = (bf16[128,2048]{1,0:T(8,128)(2,1)S(1)}, bf16[128,2048]{1,0:T(8,128)(2,1)S(1)}, u32[]{:S(2)}, u32[]{:S(2)}) collective-permute-start(bf16[128,2048]{1,0:T(8,128)(2,1)S(1)} %get-tuple-element.70), channel_id=1, source_target_pairs={{0,2},{1,3},{2,0},{3,1},{4,6},{5,7},{6,4},{7,5},{8,10},{9,11},{10,... | collective-permute-start | bytes 1572872 | tf_op jit(solution)/shard_map/ppermute | solution.py:47
  466.3 34.1 %collective-permute-start.27 = (bf16[128,2048]{1,0:T(8,128)(2,1)S(1)}, bf16[128,2048]{1,0:T(8,128)(2,1)S(1)}, u32[]{:S(2)}, u32[]{:S(2)}) collective-permute-start(bf16[128,2048]{1,0:T(8,128)(2,1)S(1)} %get-tuple-element.68), channel_id=1, source_target_pairs={{0,3},{1,0},{2,1},{3,2},{4,7},{5,4},{6,5},{7,6},{8,11},{9,8},{10,9... | collective-permute-start | bytes 1572872 | tf_op jit(solution)/shard_map/ppermute | solution.py:47
  504.7 15.0 %collective-permute-start.36 = (bf16[64,2048]{1,0:T(8,128)(2,1)}, bf16[64,2048]{1,0:T(8,128)(2,1)S(1)}, u32[]{:S(2)}, u32[]{:S(2)}) collective-permute-start(bf16[64,2048]{1,0:T(8,128)(2,1)} %get-tuple-element.97), channel_id=1, source_target_pairs={{0,16},{4,20},{8,24},{12,28},{16,0},{20,4},{24,8},{28,12},{1,17},{... | collective-permute-start | bytes 786440 | tf_op jit(solution)/shard_map/ppermute | solution.py:89
  504.7 15.1 %collective-permute-start.33 = (bf16[64,2048]{1,0:T(8,128)(2,1)}, bf16[64,2048]{1,0:T(8,128)(2,1)}, u32[]{:S(2)}, u32[]{:S(2)}) collective-permute-start(bf16[64,2048]{1,0:T(8,128)(2,1)} %get-tuple-element.96), channel_id=1, source_target_pairs={{0,8},{4,12},{8,0},{12,4},{16,24},{20,28},{24,16},{28,20},{1,9},{5... | collective-permute-start | bytes 786440 | tf_op jit(solution)/shard_map/ppermute | solution.py:89
  505.0 24.7 %collective-permute-start.35 = (bf16[64,2048]{1,0:T(8,128)(2,1)}, bf16[64,2048]{1,0:T(8,128)(2,1)}, u32[]{:S(2)}, u32[]{:S(2)}) collective-permute-start(bf16[64,2048]{1,0:T(8,128)(2,1)} %get-tuple-element.96), channel_id=1, source_target_pairs={{0,16},{4,20},{8,24},{12,28},{16,0},{20,4},{24,8},{28,12},{1,17},{... | collective-permute-start | bytes 786440 | tf_op jit(solution)/shard_map/ppermute | solution.py:89
  507.1 23.6 %collective-permute-start.34 = (bf16[64,2048]{1,0:T(8,128)(2,1)}, bf16[64,2048]{1,0:T(8,128)(2,1)}, u32[]{:S(2)}, u32[]{:S(2)}) collective-permute-start(bf16[64,2048]{1,0:T(8,128)(2,1)} %get-tuple-element.97), channel_id=1, source_target_pairs={{0,8},{4,12},{8,0},{12,4},{16,24},{20,28},{24,16},{28,20},{1,9},{5... | collective-permute-start | bytes 786440 | tf_op jit(solution)/shard_map/ppermute | solution.py:89
  519.7 15.1 %collective-permute-start.38 = (bf16[64,2048]{1,0:T(8,128)(2,1)S(1)}, bf16[64,2048]{1,0:T(8,128)(2,1)S(1)}, u32[]{:S(2)}, u32[]{:S(2)}) collective-permute-start(bf16[64,2048]{1,0:T(8,128)(2,1)S(1)} %collective-permute-done.36), channel_id=1, source_target_pairs={{0,8},{4,12},{8,0},{12,4},{16,24},{20,28},{24,16},{28,20},{1,9},{5... | collective-permute-start | bytes 786440 | tf_op jit(solution)/shard_map/ppermute | solution.py:89
  519.8 15.0 %collective-permute-start.37 = (bf16[64,2048]{1,0:T(8,128)(2,1)}, bf16[64,2048]{1,0:T(8,128)(2,1)S(1)}, u32[]{:S(2)}, u32[]{:S(2)}) collective-permute-start(bf16[64,2048]{1,0:T(8,128)(2,1)} %collective-permute-done.33), channel_id=1, source_target_pairs={{0,16},{4,20},{8,24},{12,28},{16,0},{20,4},{24,8},{28,12},{1,17},{... | collective-permute-start | bytes 786440 | tf_op jit(solution)/shard_map/ppermute | solution.py:89
  537.2 15.7 %collective-permute-start.39 = (bf16[4,128,2048]{2,1,0:T(8,128)(2,1)}, bf16[4,128,2048]{2,1,0:T(8,128)(2,1)}, u32[]{:S(2)}, u32[]{:S(2)}) collective-permute-start(bf16[4,128,2048]{2,1,0:T(8,128)(2,1)} %pad_maximum_fusion.3), channel_id=1, source_target_pairs={{0,4},{4,0},{8,12},{12,8},{16,20},{20,16},{24,28},{28,24},{1,5},{5... | collective-permute-start | bytes 6291464 | tf_op jit(solution)/shard_map/ppermute | solution.py:89
  609.9 20.0 %collective-permute-start.41 = (bf16[1024,128]{1,0:T(8,128)(2,1)}, bf16[1024,128]{1,0:T(8,128)(2,1)}, u32[]{:S(2)}, u32[]{:S(2)}) collective-permute-start(bf16[1024,128]{1,0:T(8,128)(2,1)} %bitcast.43), channel_id=1, source_target_pairs={{0,2},{1,3},{2,0},{3,1},{4,6},{5,7},{6,4},{7,5},{8,10},{9,11},{10,... | collective-permute-start | bytes 786440 | tf_op jit(solution)/shard_map/ppermute | solution.py:47
  612.3 17.6 %collective-permute-start.40 = (bf16[1024,128]{1,0:T(8,128)(2,1)}, bf16[1024,128]{1,0:T(8,128)(2,1)}, u32[]{:S(2)}, u32[]{:S(2)}) collective-permute-start(bf16[1024,128]{1,0:T(8,128)(2,1)} %bitcast.42), channel_id=1, source_target_pairs={{0,3},{1,0},{2,1},{3,2},{4,7},{5,4},{6,5},{7,6},{8,11},{9,8},{10,9... | collective-permute-start | bytes 786440 | tf_op jit(solution)/shard_map/ppermute | solution.py:47
  642.1 28.0 %collective-permute-start.43 = (bf16[4,128,2048]{2,1,0:T(8,128)(2,1)}, bf16[4,128,2048]{2,1,0:T(8,128)(2,1)}, u32[]{:S(2)}, u32[]{:S(2)}) collective-permute-start(bf16[4,128,2048]{2,1,0:T(8,128)(2,1)} %bitcast.46), channel_id=1, source_target_pairs={{0,4},{4,0},{8,12},{12,8},{16,20},{20,16},{24,28},{28,24},{1,5},{5... | collective-permute-start | bytes 6291464 | tf_op jit(solution)/shard_map/ppermute | solution.py:89
  653.2 131.2 %collective-permute-start.32 = (bf16[128,2048]{1,0:T(8,128)(2,1)}, bf16[128,2048]{1,0:T(8,128)(2,1)}, u32[]{:S(2)}, u32[]{:S(2)}) collective-permute-start(bf16[128,2048]{1,0:T(8,128)(2,1)} %get-tuple-element.66), channel_id=1, source_target_pairs={{0,1},{1,2},{2,3},{3,0},{4,5},{5,6},{6,7},{7,4},{8,9},{9,10},{10,1... | collective-permute-start | bytes 1572872 | tf_op jit(solution)/shard_map/ppermute | solution.py:47
  665.7 83.1 %all-to-all-start.2 = ((bf16[4,8,72,384]{3,2,1,0:T(8,128)(2,1)}), bf16[4,8,72,384]{3,2,1,0:T(8,128)(2,1)}, u32[]{:S(2)}, u32[]{:S(2)}) async-start(bf16[4,8,72,384]{3,2,1,0:T(8,128)(2,1)} %pad_maximum_fusion.4), calls=%async_computation.2 | async-start | bytes 3538944 | tf_op jit(solution)/shard_map/all_to_all | solution.py:52
  676.2 29.3 %collective-permute-start.50 = (bf16[64,2048]{1,0:T(8,128)(2,1)S(1)}, bf16[64,2048]{1,0:T(8,128)(2,1)S(1)}, u32[]{:S(2)}, u32[]{:S(2)}) collective-permute-start(bf16[64,2048]{1,0:T(8,128)(2,1)S(1)} %get-tuple-element.82), channel_id=1, source_target_pairs={{0,3},{1,0},{2,1},{3,2},{4,7},{5,4},{6,5},{7,6},{8,11},{9,8},{10,9... | collective-permute-start | bytes 786440 | tf_op jit(solution)/shard_map/ppermute | solution.py:59
  680.0 66.3 %collective-permute-start.49 = (bf16[64,2048]{1,0:T(8,128)(2,1)S(1)}, bf16[64,2048]{1,0:T(8,128)(2,1)S(1)}, u32[]{:S(2)}, u32[]{:S(2)}) collective-permute-start(bf16[64,2048]{1,0:T(8,128)(2,1)S(1)} %get-tuple-element.83), channel_id=1, source_target_pairs={{0,2},{1,3},{2,0},{3,1},{4,6},{5,7},{6,4},{7,5},{8,10},{9,11},{10,... | collective-permute-start | bytes 786440 | tf_op jit(solution)/shard_map/ppermute | solution.py:59
  680.0 66.3 %collective-permute-start.48 = (bf16[64,2048]{1,0:T(8,128)(2,1)S(1)}, bf16[64,2048]{1,0:T(8,128)(2,1)S(1)}, u32[]{:S(2)}, u32[]{:S(2)}) collective-permute-start(bf16[64,2048]{1,0:T(8,128)(2,1)S(1)} %get-tuple-element.81), channel_id=1, source_target_pairs={{0,1},{1,2},{2,3},{3,0},{4,5},{5,6},{6,7},{7,4},{8,9},{9,10},{10,1... | collective-permute-start | bytes 786440 | tf_op jit(solution)/shard_map/ppermute | solution.py:59
  687.9 68.0 %collective-permute-start.46 = (bf16[2,64,2048]{2,1,0:T(8,128)(2,1)}, bf16[2,64,2048]{2,1,0:T(8,128)(2,1)}, u32[]{:S(2)}, u32[]{:S(2)}) collective-permute-start(bf16[2,64,2048]{2,1,0:T(8,128)(2,1)} %stack.70), channel_id=1, source_target_pairs={{0,16},{4,20},{8,24},{12,28},{16,0},{20,4},{24,8},{28,12},{1,17},{... | collective-permute-start | bytes 1572872 | tf_op jit(solution)/shard_map/ppermute | solution.py:89
  705.5 79.0 %collective-permute-start.31 = (bf16[128,2048]{1,0:T(8,128)(2,1)}, bf16[128,2048]{1,0:T(8,128)(2,1)}, u32[]{:S(2)}, u32[]{:S(2)}) collective-permute-start(bf16[128,2048]{1,0:T(8,128)(2,1)} %get-tuple-element.67), channel_id=1, source_target_pairs={{0,2},{1,3},{2,0},{3,1},{4,6},{5,7},{6,4},{7,5},{8,10},{9,11},{10,... | collective-permute-start | bytes 1572872 | tf_op jit(solution)/shard_map/ppermute | solution.py:47
  746.3 38.1 %collective-permute-start.30 = (bf16[128,2048]{1,0:T(8,128)(2,1)}, bf16[128,2048]{1,0:T(8,128)(2,1)}, u32[]{:S(2)}, u32[]{:S(2)}) collective-permute-start(bf16[128,2048]{1,0:T(8,128)(2,1)} %get-tuple-element.65), channel_id=1, source_target_pairs={{0,3},{1,0},{2,1},{3,2},{4,7},{5,4},{6,5},{7,6},{8,11},{9,8},{10,9... | collective-permute-start | bytes 1572872 | tf_op jit(solution)/shard_map/ppermute | solution.py:47
  773.5 40.2 %all-to-all-start.4 = ((bf16[4,64,2048]{2,1,0:T(8,128)(2,1)}), bf16[4,64,2048]{2,1,0:T(8,128)(2,1)}, u32[]{:S(2)}, u32[]{:S(2)}) async-start(bf16[4,64,2048]{2,1,0:T(8,128)(2,1)} %bitcast.202), calls=%async_computation.5 | async-start | bytes 2097152 | tf_op jit(solution)/shard_map/all_to_all | solution.py:52
  782.4 23.3 %collective-permute-start.51 = (bf16[64,2048]{1,0:T(8,128)(2,1)S(1)}, bf16[64,2048]{1,0:T(8,128)(2,1)S(1)}, u32[]{:S(2)}, u32[]{:S(2)}) collective-permute-start(bf16[64,2048]{1,0:T(8,128)(2,1)S(1)} %get-tuple-element.79), channel_id=1, source_target_pairs={{0,1},{1,2},{2,3},{3,0},{4,5},{5,6},{6,7},{7,4},{8,9},{9,10},{10,1... | collective-permute-start | bytes 786440 | tf_op jit(solution)/shard_map/ppermute | solution.py:70
  788.2 35.3 %collective-permute-start.52 = (bf16[64,2048]{1,0:T(8,128)(2,1)}, bf16[64,2048]{1,0:T(8,128)(2,1)S(1)}, u32[]{:S(2)}, u32[]{:S(2)}) collective-permute-start(bf16[64,2048]{1,0:T(8,128)(2,1)} %get-tuple-element.78), channel_id=1, source_target_pairs={{0,2},{1,3},{2,0},{3,1},{4,6},{5,7},{6,4},{7,5},{8,10},{9,11},{10,... | collective-permute-start | bytes 786440 | tf_op jit(solution)/shard_map/ppermute | solution.py:70
  790.5 33.7 %collective-permute-start.53 = (bf16[64,2048]{1,0:T(8,128)(2,1)S(1)}, bf16[64,2048]{1,0:T(8,128)(2,1)S(1)}, u32[]{:S(2)}, u32[]{:S(2)}) collective-permute-start(bf16[64,2048]{1,0:T(8,128)(2,1)S(1)} %get-tuple-element.77), channel_id=1, source_target_pairs={{0,3},{1,0},{2,1},{3,2},{4,7},{5,4},{6,5},{7,6},{8,11},{9,8},{10,9... | collective-permute-start | bytes 786440 | tf_op jit(solution)/shard_map/ppermute | solution.py:70
  813.6 32.6 %all-to-all-start.5 = ((bf16[4,64,2048]{2,1,0:T(8,128)(2,1)}), bf16[4,64,2048]{2,1,0:T(8,128)(2,1)S(1)}, u32[]{:S(2)}, u32[]{:S(2)}) async-start(bf16[4,64,2048]{2,1,0:T(8,128)(2,1)} %bitcast.203), calls=%async_computation.8 | async-start | bytes 2097152 | tf_op jit(solution)/shard_map/all_to_all | solution.py:52
  (60 other events, 524.6 us)
Sparse Core Ops, SparseCore 0:
  25.3 55.3 all-gather.4
  83.1 54.5 all-gather.6
  210.9 51.4 all-gather.8
  264.8 59.2 all-gather.10
  442.7 87.3 reduce-scatter.3
  533.4 69.7 reduce-scatter.5
  606.6 71.8 reduce-scatter.7
where the time goes:
time: 864 us; the launch traced here: 855 us
  waiting for transfers between devices  335 us (39%)
  starting transfers between devices  151 us (17%)
  matrix products  96.6 us (11%)
  Pallas kernels  75.5 us (9%)
  blocking collectives  64.9 us (8%)
  other arithmetic  60.7 us (7%)
  local copies, waits for them, and re-layouts  56.3 us (7%)
  between operations  15.6 us (2%)
    dot_general x14, matrix products, mm(): return lax.dot_general(a, b, dims, preferred_element_type=F32).astype(out)  96.6 us
    ppermute x9, waiting for transfers between devices, z_gather(): parts = [x] + [lax.ppermute(x, FSDP, shift_perm(n, s)) for s in range(1, n)]  91.4 us
    ppermute x24, waiting for transfers between devices, xor_swap(): return lax.ppermute(x, CTX, [(i, i ^ bit) for i in range(n)])  77.3 us
    ppermute x9, waiting for transfers between devices, z_spread(): got = lax.ppermute(pick((me + s) % n), FSDP, shift_perm(n, s))  54.8 us
    all_to_all x1, blocking collectives, z_exchange(): return lax.all_to_all(x, FSDP, 0, 0, tiled=True)  50.9 us
    ppermute x9, waiting for transfers between devices, z_reduce(): total = total + lax.ppermute(piece, FSDP, shift_perm(n, -s)).astype(F32)  50 us
    pallas_call x1, Pallas kernels, attend_back(): pl.pallas_call(functools.partial(attend_back_body, heads=heads), out_shap...  48.3 us
    ppermute x9, starting transfers between devices, z_reduce(): total = total + lax.ppermute(piece, FSDP, shift_perm(n, -s)).astype(F32)  46.4 us
  transfers between devices with their start and end apart: 65, of which 33 were waited for; matrix products, arithmetic and copies ran while one was open for 19% of the time, Pallas kernels for 9%

commit v1 on v0

--- a/solution.py
+++ b/solution.py
@@ -76,8 +76,12 @@
     return lax.all_gather(x, CTX, axis=0, tiled=True)
 
 
-def ctx_reduce(x):
-    return lax.psum_scatter(x, CTX, scatter_dimension=0, tiled=True)
+def chip_reduce(x):
+    n = lax.axis_size(CTX)
+    groups = [list(range(core, n, 2)) for core in range(2)]
+    return lax.psum_scatter(
+        x, CTX, scatter_dimension=0, axis_index_groups=groups, tiled=True
+    )
 
 
 def xor_slots(n):
@@ -105,7 +109,8 @@
     mine = jnp.stack(
         [jnp.concatenate([half[m] for half in halves], axis=0) for m in xor_slots(n)[: n // 2]]
     )
-    return jnp.concatenate([mine, xor_swap(mine, 1)], axis=0)
+    flat = lambda y: y.reshape(-1, x.shape[1])
+    return flat(mine), flat(xor_swap(mine, 1))
 
 
 def xor_reduce(x):
@@ -267,13 +272,24 @@
         qs_ref[half] = stack_heads(q_ref[0, half], heads, False).astype(BF16)
     acc_ref[...] = jnp.zeros_like(acc_ref)
     l_ref[...] = jnp.zeros_like(l_ref)
-    for half, place, diagonal in items(meta, step, 2 * n_pairs):
+
+    def scores(half, place, diagonal):
         kv = kv_ref[:, place // 2, place % 2].reshape(n_slots * rows, LANES)
-        e = jnp.exp(lax.dot_general(qs_ref[half], kv, NT, preferred_element_type=F32))
+        return half, diagonal, kv, lax.dot_general(qs_ref[half], kv, NT, preferred_element_type=F32)
+
+    def weigh(half, diagonal, kv, s):
+        e = jnp.exp(s)
         if diagonal:
             e = jnp.where(col_ref[0:1, :] <= row_ref[:, 0:1], e, 0.0)
         l_ref[half] += lane_sums(e)
         acc_ref[half] += jnp.dot(e.astype(BF16), kv, preferred_element_type=F32)
+
+    ahead = None
+    for item in items(meta, step, 2 * n_pairs):
+        now, ahead = ahead, scores(*item)
+        if now is not None:
+            weigh(*now)
+    weigh(*ahead)
     for half in range(2):
         sums = l_ref[half]
         linv_ref[0, half : half + 1, :] = 1.0 / across(sums)
@@ -301,18 +317,29 @@
         do = stack_heads(do_ref[0, half], heads, True)
         qd_ref[half, tall:] = do.astype(BF16)
         delta_ref[half] = across(do * stack_heads(o_ref[0, half], heads, True))
-    for half, place, diagonal in items(meta, step, 2 * n_pairs):
+
+    def scores(half, place, diagonal):
         kv = kv_ref[:, place // 2, place % 2].reshape(span, LANES)
-        e = jnp.exp(lax.dot_general(kv, qd_ref[half, :tall], NT, preferred_element_type=F32))
-        p = e * linv_ref[0, pl.ds(half, 1), :]
+        s = lax.dot_general(kv, qd_ref[half, :tall], NT, preferred_element_type=F32)
+        dp = lax.dot_general(kv, qd_ref[half, tall:], NT, preferred_element_type=F32)
+        return half, place, diagonal, kv, s, dp
+
+    def gradients(half, place, diagonal, kv, s, dp):
+        p = jnp.exp(s) * linv_ref[0, pl.ds(half, 1), :]
         if diagonal:
             p = jnp.where(row_ref[:, 0:1] <= col_ref[0:1, :], p, 0.0)
-        dp = lax.dot_general(kv, qd_ref[half, tall:], NT, preferred_element_type=F32)
         ds = (p * (dp - delta_ref[half])).astype(BF16)
         dkv_acc[place] += jnp.dot(
             jnp.concatenate([ds, p.astype(BF16)], axis=1), qd_ref[half], preferred_element_type=F32
         )
         dq_acc[half] += lax.dot_general(ds, kv, TN, preferred_element_type=F32)
+
+    ahead = None
+    for item in items(meta, step, 2 * n_pairs):
+        now, ahead = ahead, scores(*item)
+        if now is not None:
+            gradients(*now)
+    gradients(*ahead)
     for half in range(2):
         for columns, tile in join_heads(dq_acc[half] * HEAD_SIZE ** (-0.5), heads, False):
             turned = rotate_tile(tile, cos_ref[0, half], -sin_ref[0, half])
@@ -390,6 +417,87 @@
     )(meta, qkv, do, o, kv_all, linv, row_pos, col_pos, cosine, sine)
 
 
+def hidden_back_body(
+    dy_ref, gate_ref, up_ref, down_ref, wg_ref, wu_ref, act_ref, dg_ref, du_ref, dn_ref, da_ref,
+    acc_ref,
+):
+    step = pl.program_id(0)
+    rows, width = acc_ref.shape
+    da_ref[...] = jnp.dot(dy_ref[...], down_ref[...], preferred_element_type=F32)
+
+    @pl.when(step == 0)
+    def _():
+        acc_ref[...] = jnp.zeros_like(acc_ref)
+
+    few = min(rows, 64)
+    for r in range(0, rows, few):
+        cut = slice(r, r + few)
+        gate, up, d_act = gate_ref[cut], up_ref[cut], da_ref[cut]
+        sigma = 1.0 / (1.0 + jnp.exp(-gate))
+        act_ref[cut] = (gate * sigma * up).astype(BF16)
+        dg_ref[cut] = (d_act * up * sigma * (1.0 + gate * (1.0 - sigma))).astype(BF16)
+        du_ref[cut] = (d_act * gate * sigma).astype(BF16)
+    some = min(width, 256)
+    for c in range(0, width, some):
+        cut = slice(c, c + some)
+        part = lax.dot_general(dg_ref[...], wg_ref[cut], NT, preferred_element_type=F32)
+        part = part + lax.dot_general(du_ref[...], wu_ref[cut], NT, preferred_element_type=F32)
+        acc_ref[:, cut] += part
+
+    @pl.when(step == pl.num_programs(0) - 1)
+    def _():
+        dn_ref[...] = acc_ref[...].astype(BF16)
+
+
+def hidden_back(dy, gate, up, down_t, gate_w, up_w):
+    rows, width = dy.shape
+    units = gate.shape[1]
+    tile = min(units, 256)
+    held = pl.BlockSpec((rows, width), lambda i: (0, 0))
+    tall = pl.BlockSpec((width, tile), lambda i: (0, i))
+    part = pl.BlockSpec((rows, tile), lambda i: (0, i))
+    return pl.pallas_call(
+        hidden_back_body,
+        out_shape=(jax.ShapeDtypeStruct((rows, units), BF16),) * 3
+        + (jax.ShapeDtypeStruct((rows, width), BF16),),
+        grid=(units // tile,),
+        in_specs=[held, part, part, tall, tall, tall],
+        out_specs=[part, part, part, held],
+        scratch_shapes=[pltpu.VMEM((rows, tile), F32), pltpu.VMEM((rows, width), F32)],
+        name="hidden_back",
+    )(dy, gate, up, down_t, gate_w, up_w)
+
+
+def core_rows_body(core, x_ref, y_ref, *refs):
+    del core
+    total = lax.dot_general(x_ref[...], y_ref[...], TN, preferred_element_type=F32)
+    for ref in refs[:-1]:
+        total = total + ref[...].astype(F32)
+    refs[-1][...] = total.astype(BF16)
+
+
+def core_rows(core, x, y, block, *addends):
+    rows, depth = x.shape
+    width = y.shape[1]
+    n_chips = depth // block // 2
+    out = pl.BlockSpec((block, width), lambda i, k: (i, 0))
+    return pl.pallas_call(
+        core_rows_body,
+        out_shape=jax.ShapeDtypeStruct((n_chips * block, width), BF16),
+        grid_spec=pltpu.PrefetchScalarGridSpec(
+            num_scalar_prefetch=1,
+            grid=(n_chips,),
+            in_specs=[
+                pl.BlockSpec((rows, block), lambda i, k: (0, 2 * i + k[0])),
+                pl.BlockSpec((rows, width), lambda i, k: (0, 0)),
+            ]
+            + [out] * len(addends),
+            out_specs=out,
+        ),
+        name="core_rows",
+    )(core, x, y, *addends)
+
+
 def shards(
     hidden_in,
     pair_order,
@@ -432,7 +540,7 @@
     in_half = jnp.arange(half_rows, dtype=jnp.int32)
     my_pos = my_fsdp * half_rows + in_half
     positions = (slot_blocks[:, :, None] * span + my_pos).reshape(plane_rows)
-    cosine, sine = rotate_tables(positions)
+    cosine, sine = lax.optimization_barrier(rotate_tables(positions))
     slot_owner = (my_fsdp - jnp.arange(n_fsdp, dtype=jnp.int32)) % n_fsdp
     key_pos = (slot_owner[:, None] * half_rows + in_half[None, :]).reshape(span)
     query_pos = jnp.tile(my_pos, heads)
@@ -463,7 +571,7 @@
     gain_one = all_gains[:, :, :weight_rows].reshape(1, model_width)
     gain_two = all_gains[:, :, weight_rows:].reshape(1, model_width)
 
-    hidden_all = xor_gather(hidden_in).reshape(plane_rows, model_width)
+    hidden_all = jnp.concatenate(xor_gather(hidden_in), axis=0)
     normed_one, qkv, w_qkv = project(
         hidden_all, gain_one, w_first, cosine, sine, query_width, weight_rows
     )
@@ -504,23 +612,23 @@
 
     gate_proj = mm(normed_two, gate_w)
     up_proj = mm(normed_two, up_w)
-    gate_proj, up_proj = lax.optimization_barrier((gate_proj, up_proj))
-    d_act = mm(grad_all, down_t)
-    sigmoid_gate = jax.nn.sigmoid(gate_proj)
-    activated = (gate_proj * sigmoid_gate * up_proj).astype(BF16)
-    d_gate = (d_act * up_proj * sigmoid_gate * (1.0 + gate_proj * (1.0 - sigmoid_gate))).astype(
-        BF16
-    )
-    d_up = (d_act * gate_proj * sigmoid_gate).astype(BF16)
-    d_normed_partial = (mm(d_gate, gate_w, NT) + mm(d_up, up_w, NT)).astype(BF16)
+    activated, d_gate, d_up, d_normed_partial = hidden_back(
+        grad_all, gate_proj, up_proj, down_t, gate_w, up_w
+    )
     d_normed_two = z_reduce(d_normed_partial)
 
-    ffn_partials = [
-        mm(after(grad_all, d_normed_partial), activated, TN, BF16),
-        mm(after(normed_two, d_normed_partial), d_gate, TN, BF16),
-        mm(after(normed_two, d_normed_partial), d_up, TN, BF16),
-    ]
-    ffn_grads = [ctx_reduce(g) for g in ffn_partials]
+    block = n_fsdp * weight_rows
+    core = (my_ctx % 2).reshape(1)
+    normed_late = after(normed_two, d_normed_partial)
+    factors = (
+        (after(grad_all, d_normed_partial), activated),
+        (normed_late, d_gate),
+        (normed_late, d_up),
+    )
+    away = [core_rows(1 - core, x, y, block) for x, y in factors]
+    got = [xor_swap(x, 1) for x in away]
+    ffn_partials = [core_rows(core, x, y, block, z) for (x, y), z in zip(factors, got)]
+    ffn_grads = [chip_reduce(g) for g in ffn_partials]
     result_partial = mm(after(activated, d_normed_two), down_t, NT, BF16)
     result = after_attn + z_reduce(after(result_partial, d_normed_two))
 
@@ -529,10 +637,14 @@
     d_mixed = out_grad.astype(F32) + scale_two * (
         d_unit_two - unit_two * jnp.mean(d_unit_two * unit_two, axis=1, keepdims=True)
     )
-    d_attn = xor_gather(d_mixed.astype(BF16)).reshape(plane_rows, model_width)
-    d_attn = after(d_attn, *ffn_partials)
-    d_o = mm(d_attn, w_out_slice, NT, BF16)
-    out_partial = mm(o_b, d_attn, TN, BF16).reshape(n_fsdp, weight_rows, model_width)
+    d_mine, d_other = xor_gather(d_mixed.astype(BF16))
+    d_mine = after(d_mine, *ffn_partials)
+    d_o = jnp.concatenate(
+        [mm(d_mine, w_out_slice, NT, BF16), mm(d_other, w_out_slice, NT, BF16)], axis=0
+    )
+    middle = plane_rows // 2
+    out_partial = mm(o_b[:middle], d_mine, TN) + mm(o_b[middle:], d_other, TN)
+    out_partial = out_partial.astype(BF16).reshape(n_fsdp, weight_rows, model_width)
     grad_out_w = z_sum(lambda d: lax.dynamic_index_in_dim(out_partial, d, 0, False))
     pair_view = lambda x: x.reshape(n_ctx, 2, half_rows, -1)
     dq, dkv_all = attend_back(
@@ -592,9 +704,9 @@
 
     homes = [g.reshape(n_fsdp, weight_rows, unit_slice) for g in ffn_grads]
     down_sum = columns_home(z_exchange(homes[0]))
-    gate_sum = columns_home(z_exchange(homes[1]))
-    up_pick = lambda d: lax.dynamic_index_in_dim(homes[2], d, 0, False)
-    up_sum = columns_home(z_spread(up_pick))
+    pick_of = lambda home: lambda d: lax.dynamic_index_in_dim(home, d, 0, False)
+    gate_sum = columns_home(z_spread(pick_of(homes[1])))
+    up_sum = columns_home(z_spread(pick_of(homes[2])))
     return (
         result,
         grad_in,

time: 864 us -> 867 us (level)
  Pallas kernels: 75.5 us -> 130 us
  matrix products: 96.6 us -> 51.4 us
  other arithmetic: 60.7 us -> 49.3 us
    pallas_call x0 -> x7, Pallas kernels: none -> 70.4 us  [the longest x6 40.3 us: core_rows(): pl.pallas_call(core_rows_body, out_shape=jax.ShapeDtypeStruct((n_chips *...]
    dot_general x14 -> x10, matrix products: 96.6 us -> 51.4 us  [mm(): return lax.dot_general(a, b, dims, preferred_element_type=F32).astype(out)]
    pallas_call x1, Pallas kernels: 48.3 us -> 33 us  [attend_back(): pl.pallas_call(functools.partial(attend_back_body, heads=heads), out_shap...]
    all_to_all x3 -> x2, waiting for transfers between devices: 22.6 us -> 8.41 us  [z_exchange(): return lax.all_to_all(x, FSDP, 0, 0, tiled=True)]
    ppermute x9, waiting for transfers between devices: 91.4 us -> 77.8 us  [z_gather(): parts = [x] + [lax.ppermute(x, FSDP, shift_perm(n, s)) for s in range(1, n)]]
    ppermute x24 -> x27, waiting for transfers between devices: 77.3 us -> 90.6 us  [xor_swap(): return lax.ppermute(x, CTX, [(i, i ^ bit) for i in range(n)])]
    ppermute x9 -> x12, waiting for transfers between devices: 54.8 us -> 66.5 us  [z_spread(): got = lax.ppermute(pick((me + s) % n), FSDP, shift_perm(n, s))]
    all_to_all x3 -> x2, starting transfers between devices: 18.5 us -> 10.4 us  [z_exchange(): return lax.all_to_all(x, FSDP, 0, 0, tiled=True)]
  transfers between devices with their start and end apart: 65 -> 70, of which waited for: 33 -> 39; matrix products, arithmetic and copies ran while one was open for 19% -> 17% of each run, Pallas kernels for 9% -> 10%
where the time goes in v1:
time: 867 us; the launch traced here: 855 us
  waiting for transfers between devices  339 us (39%)
  starting transfers between devices  146 us (17%)
  Pallas kernels  130 us (15%)
  blocking collectives  71.9 us (8%)
  matrix products  51.4 us (6%)
  local copies, waits for them, and re-layouts  51.2 us (6%)
  other arithmetic  49.3 us (6%)
  between operations  15.3 us (2%)
    ppermute x27, waiting for transfers between devices, xor_swap(): return lax.ppermute(x, CTX, [(i, i ^ bit) for i in range(n)])  90.6 us
    ppermute x9, waiting for transfers between devices, z_gather(): parts = [x] + [lax.ppermute(x, FSDP, shift_perm(n, s)) for s in range(1, n)]  77.8 us
    ppermute x12, waiting for transfers between devices, z_spread(): got = lax.ppermute(pick((me + s) % n), FSDP, shift_perm(n, s))  66.5 us
    ppermute x9, waiting for transfers between devices, z_reduce(): total = total + lax.ppermute(piece, FSDP, shift_perm(n, -s)).astype(F32)  58.4 us
    all_to_all x1, blocking collectives, z_exchange(): return lax.all_to_all(x, FSDP, 0, 0, tiled=True)  58 us
    dot_general x10, matrix products, mm(): return lax.dot_general(a, b, dims, preferred_element_type=F32).astype(out)  51.4 us
    ppermute x9, starting transfers between devices, z_reduce(): total = total + lax.ppermute(piece, FSDP, shift_perm(n, -s)).astype(F32)  45.1 us
    pallas_call x6, Pallas kernels, core_rows(): pl.pallas_call(core_rows_body, out_shape=jax.ShapeDtypeStruct((n_chips *...  40.3 us
  transfers between devices with their start and end apart: 70, of which 39 were waited for; matrix products, arithmetic and copies ran while one was open for 17% of the time, Pallas kernels for 10%

profile of v1, /device:TPU:0, one launch (start us, length us, event | category | flops | bytes accessed | tf_op | source)
XLA Modules:
  0.0 854.9 jit_solution(6836515856260819919)
XLA Ops:
  11.2 13.9 %all_to_all.25 = bf16[8,72,384]{2,1,0:T(8,128)(2,1)} all-to-all(bf16[8,72,384]{2,1,0:T(8,128)(2,1)S(1)} %pad_maximum_fusion.13), channel_id=1, replica_groups=mesh['ctx'=8,'fsdp'=4] {'ctx'}, dimensions={0} | all-to-all | bytes 884736 | tf_op jit(solution)/shard_map/all_to_all | solution.py:567
  31.1 5.6 collective-permute-done.10
  37.6 20.5 %collective-permute-done.11 = bf16[64,2048]{1,0:T(8,128)(2,1)} collective-permute-done((bf16[64,2048]{1,0:T(8,128)(2,1)S(1)}, bf16[64,2048]{1,0:T(8,128)(2,1)}, u32[]{:S(2)}, u32[]{:S(2)}) %collective-permute-start.11) | collective-permute-done | bytes 262176 | tf_op jit(solution)/shard_map/ppermute | solution.py:70
  65.2 5.1 collective-permute-done
  94.4 7.9 project.1
  103.2 22.0 %collective-permute-start.7 = (bf16[1024,128]{1,0:T(8,128)(2,1)S(1)}, bf16[1024,128]{1,0:T(8,128)(2,1)S(1)}, u32[]{:S(2)}, u32[]{:S(2)}) collective-permute-start(bf16[1024,128]{1,0:T(8,128)(2,1)S(1)} %slice.198), channel_id=1, source_target_pairs={{0,1},{1,2},{2,3},{3,0},{4,5},{5,6},{6,7},{7,4},{8,9},{9,10},{10,1... | collective-permute-start | bytes 786440 | tf_op jit(solution)/shard_map/ppermute | solution.py:37
  131.9 8.1 collective-permute-done.8
  143.7 58.0 %all_to_all.26 = bf16[4,64,4096]{2,1,0:T(8,128)(2,1)S(1)} all-to-all(bf16[4,64,4096]{2,1,0:T(8,128)(2,1)S(1)} %pad_maximum_fusion.2), channel_id=1, replica_groups=mesh['ctx'=8,'fsdp'=4] {'fsdp'}, dimensions={0} | all-to-all | bytes 4194304 | tf_op jit(solution)/shard_map/all_to_all | solution.py:52
  209.0 5.4 collective-permute-done.13
  214.4 9.4 %collective-permute-done.14 = bf16[64,2048]{1,0:T(8,128)(2,1)S(1)} collective-permute-done((bf16[64,2048]{1,0:T(8,128)(2,1)S(1)}, bf16[64,2048]{1,0:T(8,128)(2,1)S(1)}, u32[]{:S(2)}, u32[]{:S(2)}) %collective-permute-start.14) | collective-permute-done | bytes 262176 | tf_op jit(solution)/shard_map/ppermute | solution.py:70
  225.4 16.4 %attend.1 = (f32[8,2,64,256]{3,2,1,0:T(8,128)}, bf16[8,2,64,256]{3,2,1,0:T(8,128)(2,1)}, f32[8,2,256]{2,1,0:T(2,128)}) custom-call(s32[24]{0:T(128)} %pad_add_fusion.1.meta, bf16[8,2,64,384]{3,2,1,0:T(8,128)(2,1)} %bitcast.189, bf16[4,8,2,64,128]{4,3,2,1,0:T(8,128)(2,1)} %bitcast.181, s32[256,128]{1,0:T(8,128)} %broadcast_in_dim.135.row_ref, ...), custom_call_target="tpu_custom_call" | custom-call | tf_op jit(solution)/shard_map/attend/pallas_call | solution.py:368
  251.8 13.4 %collective-permute-done.17 = bf16[2,64,2048]{2,1,0:T(8,128)(2,1)S(1)} collective-permute-done((bf16[2,64,2048]{2,1,0:T(8,128)(2,1)S(1)}, bf16[2,64,2048]{2,1,0:T(8,128)(2,1)S(1)}, u32[]{:S(2)}, u32[]{:S(2)}) %collective-permute-start.17) | collective-permute-done | bytes 524320 | tf_op jit(solution)/shard_map/ppermute | solution.py:93
  266.8 12.2 %collective-permute-done.18 = bf16[1,64,2048]{2,1,0:T(8,128)(2,1)S(1)} collective-permute-done((bf16[1,64,2048]{2,1,0:T(8,128)(2,1)S(1)}, bf16[1,64,2048]{2,1,0:T(8,128)(2,1)S(1)}, u32[]{:S(2)}, u32[]{:S(2)}) %collective-permute-start.18) | collective-permute-done | bytes 262176 | tf_op jit(solution)/shard_map/ppermute | solution.py:93
  279.9 7.0 collective-permute-done.20
  289.2 6.8 collective-permute-start.24
  302.0 6.6 collective-permute-done.24
  310.0 18.8 %collective-permute-done.25 = bf16[128,2048]{1,0:T(8,128)(2,1)} collective-permute-done((bf16[128,2048]{1,0:T(8,128)(2,1)}, bf16[128,2048]{1,0:T(8,128)(2,1)}, u32[]{:S(2)}, u32[]{:S(2)}) %collective-permute-start.25) | collective-permute-done | bytes 524320 | tf_op jit(solution)/shard_map/ppermute | solution.py:37
  334.2 8.2 collective-permute-done.21
  343.4 27.1 %collective-permute-done.22 = bf16[128,2048]{1,0:T(8,128)(2,1)S(1)} collective-permute-done((bf16[128,2048]{1,0:T(8,128)(2,1)}, bf16[128,2048]{1,0:T(8,128)(2,1)S(1)}, u32[]{:S(2)}, u32[]{:S(2)}) %collective-permute-start.22) | collective-permute-done | bytes 524320 | tf_op jit(solution)/shard_map/ppermute | solution.py:37
  370.7 11.2 %fusion.31.gate_ref = f32[512,2048]{1,0:T(8,128)} fusion(bf16[2048,2048]{1,0:T(8,128)(2,1)} %all-gather.7.cloned.1.call-done.wg_ref, bf16[128,2048]{1,0:T(8,128)(2,1)} %collective-permute-done.26, bf16[128,2048]{1,0:T(8,128)(2,1)} %collective-permute-done.25, bf16[128,2048]{1,0:T(8,128)(2,1)} %collective-permute-done.24, ...), kind=kOutput, calls=%fused_computation.159 | convolution fusion | flops 4303355904 | bytes 14680064 | tf_op jit(solution)/shard_map/dot_general | solution.py:28
  381.9 10.5 %fusion.30.up_ref = f32[512,2048]{1,0:T(8,128)} fusion(bf16[2048,2048]{1,0:T(8,128)(2,1)} %all-gather.9.cloned.1.call-done.wu_ref, bf16[128,2048]{1,0:T(8,128)(2,1)} %collective-permute-done.26, bf16[128,2048]{1,0:T(8,128)(2,1)} %collective-permute-done.25, bf16[128,2048]{1,0:T(8,128)(2,1)} %collective-permute-done.24, ...), kind=kOutput, calls=%fused_computation.158 | convolution fusion | flops 4303355904 | bytes 14680064 | tf_op jit(solution)/shard_map/dot_general | solution.py:28
  392.3 30.1 %hidden_back.1 = (bf16[512,2048]{1,0:T(8,128)(2,1)}, bf16[512,2048]{1,0:T(8,128)(2,1)}, bf16[512,2048]{1,0:T(8,128)(2,1)}, bf16[512,2048]{1,0:T(8,128)(2,1)}) custom-call(bf16[512,2048]{1,0:T(8,128)(2,1)} %copy-done, f32[512,2048]{1,0:T(8,128)} %fusion.31.gate_ref, f32[512,2048]{1,0:T(8,128)} %fusion.30.up_ref, ...), custom_call_target="tpu_custom_call" | custom-call | tf_op jit(solution)/shard_map/hidden_back/pallas_call | solution.py:459
  422.4 6.3 core_rows.10
  428.7 7.5 collective-permute-done.41.refs_0_
  436.2 7.0 core_rows.11
  443.3 6.3 core_rows.8
  449.7 7.4 collective-permute-done.40.refs_0_
  457.1 7.3 core_rows.9
  467.2 14.8 %collective-permute-start.27 = (bf16[128,2048]{1,0:T(8,128)(2,1)}, bf16[128,2048]{1,0:T(8,128)(2,1)}, u32[]{:S(2)}, u32[]{:S(2)}) collective-permute-start(bf16[128,2048]{1,0:T(8,128)(2,1)} %get-tuple-element.71), channel_id=1, source_target_pairs={{0,3},{1,0},{2,1},{3,2},{4,7},{5,4},{6,5},{7,6},{8,11},{9,8},{10,9... | collective-permute-start | bytes 1572872 | tf_op jit(solution)/shard_map/ppermute | solution.py:47
  482.7 6.3 core_rows.6
  489.0 5.7 collective-permute-done.27
  494.7 32.0 %collective-permute-done.28 = bf16[128,2048]{1,0:T(8,128)(2,1)} collective-permute-done((bf16[128,2048]{1,0:T(8,128)(2,1)}, bf16[128,2048]{1,0:T(8,128)(2,1)}, u32[]{:S(2)}, u32[]{:S(2)}) %collective-permute-start.28) | collective-permute-done | bytes 524320 | tf_op jit(solution)/shard_map/ppermute | solution.py:47
  534.9 10.5 %collective-permute-done.33 = bf16[64,2048]{1,0:T(8,128)(2,1)S(1)} collective-permute-done((bf16[64,2048]{1,0:T(8,128)(2,1)S(1)}, bf16[64,2048]{1,0:T(8,128)(2,1)S(1)}, u32[]{:S(2)}, u32[]{:S(2)}) %collective-permute-start.33) | collective-permute-done | bytes 262176 | tf_op jit(solution)/shard_map/ppermute | solution.py:93
  548.2 5.3 collective-permute-done.34
  553.7 5.0 collective-permute-done.37
  568.0 7.1 core_rows.7
  579.9 33.0 %attend_back.1 = (bf16[8,2,64,256]{3,2,1,0:T(8,128)(2,1)}, bf16[4,8,2,64,128]{4,3,2,1,0:T(8,128)(2,1)}) custom-call(s32[24]{0:T(128)} %pad_add_fusion.1.meta, bf16[8,2,64,384]{3,2,1,0:T(8,128)(2,1)} %bitcast.190, bf16[8,2,64,256]{3,2,1,0:T(8,128)(2,1)} %bitcast.200, f32[8,2,64,256]{3,2,1,0:T(8,128)} %get-tuple-element.49.o_ref, ...), custom_call_target="tpu_custom_call" | custom-call | tf_op jit(solution)/shard_map/attend_back/pallas_call | solution.py:395
  625.7 16.0 %collective-permute-done.44 = bf16[1024,128]{1,0:T(8,128)(2,1)} collective-permute-done((bf16[1024,128]{1,0:T(8,128)(2,1)}, bf16[1024,128]{1,0:T(8,128)(2,1)}, u32[]{:S(2)}, u32[]{:S(2)}) %collective-permute-start.44) | collective-permute-done | bytes 262176 | tf_op jit(solution)/shard_map/ppermute | solution.py:47
  653.6 8.1 convolution_convert_fusion.2
  671.3 5.3 all-to-all-start.2
  694.9 21.5 %collective-permute-done.51 = bf16[64,2048]{1,0:T(8,128)(2,1)S(1)} collective-permute-done((bf16[64,2048]{1,0:T(8,128)(2,1)S(1)}, bf16[64,2048]{1,0:T(8,128)(2,1)S(1)}, u32[]{:S(2)}, u32[]{:S(2)}) %collective-permute-start.51) | collective-permute-done | bytes 262176 | tf_op jit(solution)/shard_map/ppermute | solution.py:59
  716.4 20.3 %collective-permute-start.31 = (bf16[128,2048]{1,0:T(8,128)(2,1)}, bf16[128,2048]{1,0:T(8,128)(2,1)}, u32[]{:S(2)}, u32[]{:S(2)}) collective-permute-start(bf16[128,2048]{1,0:T(8,128)(2,1)} %get-tuple-element.70), channel_id=1, source_target_pairs={{0,2},{1,3},{2,0},{3,1},{4,6},{5,7},{6,4},{7,5},{8,10},{9,11},{10,... | collective-permute-start | bytes 1572872 | tf_op jit(solution)/shard_map/ppermute | solution.py:47
  736.7 10.6 %collective-permute-done.52 = bf16[64,2048]{1,0:T(8,128)(2,1)S(1)} collective-permute-done((bf16[64,2048]{1,0:T(8,128)(2,1)S(1)}, bf16[64,2048]{1,0:T(8,128)(2,1)S(1)}, u32[]{:S(2)}, u32[]{:S(2)}) %collective-permute-start.52) | collective-permute-done | bytes 262176 | tf_op jit(solution)/shard_map/ppermute | solution.py:59
  764.3 5.4 all-to-all-done.3
  792.4 5.1 all-to-all-start.4
  802.9 13.1 %collective-permute-done.58 = bf16[64,2048]{1,0:T(8,128)(2,1)} collective-permute-done((bf16[64,2048]{1,0:T(8,128)(2,1)}, bf16[64,2048]{1,0:T(8,128)(2,1)}, u32[]{:S(2)}, u32[]{:S(2)}) %collective-permute-start.58) | collective-permute-done | bytes 262176 | tf_op jit(solution)/shard_map/ppermute | solution.py:70
  822.3 12.6 %collective-permute-done.55 = bf16[64,2048]{1,0:T(8,128)(2,1)} collective-permute-done((bf16[64,2048]{1,0:T(8,128)(2,1)S(1)}, bf16[64,2048]{1,0:T(8,128)(2,1)}, u32[]{:S(2)}, u32[]{:S(2)}) %collective-permute-start.55) | collective-permute-done | bytes 262176 | tf_op jit(solution)/shard_map/ppermute | solution.py:70
  837.7 8.4 all-to-all-done.4
  (318 shorter events, 228.0 us)
Async XLA Ops:
  7.2 85.6 %all-gather.5.cloned.1.call-start = ((), (), s32[]{:S(2)}) async-start(), calls=%async_computation.8 | async-start | bytes 2211840 | tf_op jit(solution)/shard_map/all_gather | solution.py:568
  25.1 345.5 %all-gather.7.cloned.1.call-start = ((), (), s32[]{:S(2)}) async-start(), calls=%async_computation.9 | async-start | bytes 9437184 | tf_op jit(solution)/shard_map/all_gather | solution.py:76
  27.0 31.1 %collective-permute-start.11 = (bf16[64,2048]{1,0:T(8,128)(2,1)S(1)}, bf16[64,2048]{1,0:T(8,128)(2,1)}, u32[]{:S(2)}, u32[]{:S(2)}) collective-permute-start(bf16[64,2048]{1,0:T(8,128)(2,1)S(1)} %get-tuple-element.99), channel_id=1, source_target_pairs={{0,2},{1,3},{2,0},{3,1},{4,6},{5,7},{6,4},{7,5},{8,10},{9,11},{10,... | collective-permute-start | bytes 786440 | tf_op jit(solution)/shard_map/ppermute | solution.py:70
  29.6 29.5 %collective-permute-start.12 = (bf16[64,2048]{1,0:T(8,128)(2,1)S(1)}, bf16[64,2048]{1,0:T(8,128)(2,1)}, u32[]{:S(2)}, u32[]{:S(2)}) collective-permute-start(bf16[64,2048]{1,0:T(8,128)(2,1)S(1)} %get-tuple-element.97), channel_id=1, source_target_pairs={{0,3},{1,0},{2,1},{3,2},{4,7},{5,4},{6,5},{7,6},{8,11},{9,8},{10,9... | collective-permute-start | bytes 786440 | tf_op jit(solution)/shard_map/ppermute | solution.py:70
  61.0 320.8 %all-gather.9.cloned.1.call-start = ((), (), s32[]{:S(2)}) async-start(), calls=%async_computation.10 | async-start | bytes 9437184 | tf_op jit(solution)/shard_map/all_gather | solution.py:76
  103.2 28.7 %collective-permute-start.7 = (bf16[1024,128]{1,0:T(8,128)(2,1)S(1)}, bf16[1024,128]{1,0:T(8,128)(2,1)S(1)}, u32[]{:S(2)}, u32[]{:S(2)}) collective-permute-start(bf16[1024,128]{1,0:T(8,128)(2,1)S(1)} %slice.198), channel_id=1, source_target_pairs={{0,1},{1,2},{2,3},{3,0},{4,5},{5,6},{6,7},{7,4},{8,9},{9,10},{10,1... | collective-permute-start | bytes 786440 | tf_op jit(solution)/shard_map/ppermute | solution.py:37
  125.2 14.8 %collective-permute-start.8 = (bf16[1024,128]{1,0:T(8,128)(2,1)S(1)}, bf16[1024,128]{1,0:T(8,128)(2,1)S(1)}, u32[]{:S(2)}, u32[]{:S(2)}) collective-permute-start(bf16[1024,128]{1,0:T(8,128)(2,1)S(1)} %slice.198), channel_id=1, source_target_pairs={{0,2},{1,3},{2,0},{3,1},{4,6},{5,7},{6,4},{7,5},{8,10},{9,11},{10,... | collective-permute-start | bytes 786440 | tf_op jit(solution)/shard_map/ppermute | solution.py:37
  125.2 17.5 %collective-permute-start.9 = (bf16[1024,128]{1,0:T(8,128)(2,1)S(1)}, bf16[1024,128]{1,0:T(8,128)(2,1)S(1)}, u32[]{:S(2)}, u32[]{:S(2)}) collective-permute-start(bf16[1024,128]{1,0:T(8,128)(2,1)S(1)} %slice.198), channel_id=1, source_target_pairs={{0,3},{1,0},{2,1},{3,2},{4,7},{5,4},{6,5},{7,6},{8,11},{9,8},{10,9... | collective-permute-start | bytes 786440 | tf_op jit(solution)/shard_map/ppermute | solution.py:37
  203.2 189.1 %all-gather.11.cloned.1.call-start = ((), (), s32[]{:S(2)}) async-start(), calls=%async_computation.11 | async-start | bytes 9437184 | tf_op jit(solution)/shard_map/all_gather | solution.py:76
  203.5 20.3 %collective-permute-start.14 = (bf16[64,2048]{1,0:T(8,128)(2,1)S(1)}, bf16[64,2048]{1,0:T(8,128)(2,1)S(1)}, u32[]{:S(2)}, u32[]{:S(2)}) collective-permute-start(bf16[64,2048]{1,0:T(8,128)(2,1)S(1)} %copy-done.23), channel_id=1, source_target_pairs={{0,2},{1,3},{2,0},{3,1},{4,6},{5,7},{6,4},{7,5},{8,10},{9,11},{10,... | collective-permute-start | bytes 786440 | tf_op jit(solution)/shard_map/ppermute | solution.py:70
  205.5 18.4 %collective-permute-start.15 = (bf16[64,2048]{1,0:T(8,128)(2,1)S(1)}, bf16[64,2048]{1,0:T(8,128)(2,1)S(1)}, u32[]{:S(2)}, u32[]{:S(2)}) collective-permute-start(bf16[64,2048]{1,0:T(8,128)(2,1)S(1)} %copy-done.23), channel_id=1, source_target_pairs={{0,3},{1,0},{2,1},{3,2},{4,7},{5,4},{6,5},{7,6},{8,11},{9,8},{10,9... | collective-permute-start | bytes 786440 | tf_op jit(solution)/shard_map/ppermute | solution.py:70
  207.2 569.7 %reduce-scatter.6.cloned.1.call-start = ((), (), s32[]{:S(2)}) async-start(), calls=%async_computation.13 | async-start | bytes 5242880 | tf_op jit(solution)/shard_map/reduce_scatter | solution.py:82
  250.1 15.0 %collective-permute-start.17 = (bf16[2,64,2048]{2,1,0:T(8,128)(2,1)S(1)}, bf16[2,64,2048]{2,1,0:T(8,128)(2,1)S(1)}, u32[]{:S(2)}, u32[]{:S(2)}) collective-permute-start(bf16[2,64,2048]{2,1,0:T(8,128)(2,1)S(1)} %pad_maximum_fusion.8), channel_id=1, source_target_pairs={{0,8},{4,12},{8,0},{12,4},{16,24},{20,28},{24,16},{28,20},{1,9},{5... | collective-permute-start | bytes 1572872 | tf_op jit(solution)/shard_map/ppermute | solution.py:93
  251.7 15.1 %collective-permute-start.19 = (bf16[2,64,2048]{2,1,0:T(8,128)(2,1)S(1)}, bf16[2,64,2048]{2,1,0:T(8,128)(2,1)S(1)}, u32[]{:S(2)}, u32[]{:S(2)}) collective-permute-start(bf16[2,64,2048]{2,1,0:T(8,128)(2,1)S(1)} %stack.69), channel_id=1, source_target_pairs={{0,16},{4,20},{8,24},{12,28},{16,0},{20,4},{24,8},{28,12},{1,17},{... | collective-permute-start | bytes 1572872 | tf_op jit(solution)/shard_map/ppermute | solution.py:93
  289.2 19.4 %collective-permute-start.24 = (bf16[128,2048]{1,0:T(8,128)(2,1)}, bf16[128,2048]{1,0:T(8,128)(2,1)}, u32[]{:S(2)}, u32[]{:S(2)}) collective-permute-start(bf16[128,2048]{1,0:T(8,128)(2,1)} %multiply_convert_fusion), channel_id=1, source_target_pairs={{0,1},{1,2},{2,3},{3,0},{4,5},{5,6},{6,7},{7,4},{8,9},{9,10},{10,1... | collective-permute-start | bytes 1572872 | tf_op jit(solution)/shard_map/ppermute | solution.py:37
  296.0 32.8 %collective-permute-start.25 = (bf16[128,2048]{1,0:T(8,128)(2,1)}, bf16[128,2048]{1,0:T(8,128)(2,1)}, u32[]{:S(2)}, u32[]{:S(2)}) collective-permute-start(bf16[128,2048]{1,0:T(8,128)(2,1)} %multiply_convert_fusion), channel_id=1, source_target_pairs={{0,2},{1,3},{2,0},{3,1},{4,6},{5,7},{6,4},{7,5},{8,10},{9,11},{10,... | collective-permute-start | bytes 1572872 | tf_op jit(solution)/shard_map/ppermute | solution.py:37
  296.0 35.1 %collective-permute-start.26 = (bf16[128,2048]{1,0:T(8,128)(2,1)}, bf16[128,2048]{1,0:T(8,128)(2,1)}, u32[]{:S(2)}, u32[]{:S(2)}) collective-permute-start(bf16[128,2048]{1,0:T(8,128)(2,1)} %multiply_convert_fusion), channel_id=1, source_target_pairs={{0,3},{1,0},{2,1},{3,2},{4,7},{5,4},{6,5},{7,6},{8,11},{9,8},{10,9... | collective-permute-start | bytes 1572872 | tf_op jit(solution)/shard_map/ppermute | solution.py:37
  298.3 44.0 %collective-permute-start.21 = (bf16[128,2048]{1,0:T(8,128)(2,1)}, bf16[128,2048]{1,0:T(8,128)(2,1)}, u32[]{:S(2)}, u32[]{:S(2)}) collective-permute-start(bf16[128,2048]{1,0:T(8,128)(2,1)} %param.24), channel_id=1, source_target_pairs={{0,1},{1,2},{2,3},{3,0},{4,5},{5,6},{6,7},{7,4},{8,9},{9,10},{10,1... | collective-permute-start | bytes 1572872 | tf_op jit(solution)/shard_map/ppermute | solution.py:37
  298.3 72.2 %collective-permute-start.22 = (bf16[128,2048]{1,0:T(8,128)(2,1)}, bf16[128,2048]{1,0:T(8,128)(2,1)S(1)}, u32[]{:S(2)}, u32[]{:S(2)}) collective-permute-start(bf16[128,2048]{1,0:T(8,128)(2,1)} %param.24), channel_id=1, source_target_pairs={{0,2},{1,3},{2,0},{3,1},{4,6},{5,7},{6,4},{7,5},{8,10},{9,11},{10,... | collective-permute-start | bytes 1572872 | tf_op jit(solution)/shard_map/ppermute | solution.py:37
  308.6 62.0 %collective-permute-start.23 = (bf16[128,2048]{1,0:T(8,128)(2,1)}, bf16[128,2048]{1,0:T(8,128)(2,1)S(1)}, u32[]{:S(2)}, u32[]{:S(2)}) collective-permute-start(bf16[128,2048]{1,0:T(8,128)(2,1)} %param.24), channel_id=1, source_target_pairs={{0,3},{1,0},{2,1},{3,2},{4,7},{5,4},{6,5},{7,6},{8,11},{9,8},{10,9... | collective-permute-start | bytes 1572872 | tf_op jit(solution)/shard_map/ppermute | solution.py:37
  443.2 347.1 %reduce-scatter.4.cloned.1.call-start = ((), (), s32[]{:S(2)}) async-start(), calls=%async_computation.12 | async-start | bytes 5242880 | tf_op jit(solution)/shard_map/reduce_scatter | solution.py:82
  464.4 327.9 %reduce-scatter.8.cloned.1.call-start = ((), (), s32[]{:S(2)}) async-start(), calls=%async_computation.14 | async-start | bytes 5242880 | tf_op jit(solution)/shard_map/reduce_scatter | solution.py:82
  467.2 27.5 %collective-permute-start.27 = (bf16[128,2048]{1,0:T(8,128)(2,1)}, bf16[128,2048]{1,0:T(8,128)(2,1)}, u32[]{:S(2)}, u32[]{:S(2)}) collective-permute-start(bf16[128,2048]{1,0:T(8,128)(2,1)} %get-tuple-element.71), channel_id=1, source_target_pairs={{0,3},{1,0},{2,1},{3,2},{4,7},{5,4},{6,5},{7,6},{8,11},{9,8},{10,9... | collective-permute-start | bytes 1572872 | tf_op jit(solution)/shard_map/ppermute | solution.py:47
  482.0 44.7 %collective-permute-start.28 = (bf16[128,2048]{1,0:T(8,128)(2,1)}, bf16[128,2048]{1,0:T(8,128)(2,1)}, u32[]{:S(2)}, u32[]{:S(2)}) collective-permute-start(bf16[128,2048]{1,0:T(8,128)(2,1)} %get-tuple-element.73), channel_id=1, source_target_pairs={{0,2},{1,3},{2,0},{3,1},{4,6},{5,7},{6,4},{7,5},{8,10},{9,11},{10,... | collective-permute-start | bytes 1572872 | tf_op jit(solution)/shard_map/ppermute | solution.py:47
  482.0 44.7 %collective-permute-start.29 = (bf16[128,2048]{1,0:T(8,128)(2,1)}, bf16[128,2048]{1,0:T(8,128)(2,1)}, u32[]{:S(2)}, u32[]{:S(2)}) collective-permute-start(bf16[128,2048]{1,0:T(8,128)(2,1)} %get-tuple-element.72), channel_id=1, source_target_pairs={{0,1},{1,2},{2,3},{3,0},{4,5},{5,6},{6,7},{7,4},{8,9},{9,10},{10,1... | collective-permute-start | bytes 1572872 | tf_op jit(solution)/shard_map/ppermute | solution.py:47
  489.0 79.0 %collective-permute-start.39 = (bf16[1024,2048]{1,0:T(8,128)(2,1)}, bf16[1024,2048]{1,0:T(8,128)(2,1)}, u32[]{:S(2)}, u32[]{:S(2)}) collective-permute-start(bf16[1024,2048]{1,0:T(8,128)(2,1)} %core_rows.6), channel_id=1, source_target_pairs={{0,4},{4,0},{8,12},{12,8},{16,20},{20,16},{24,28},{28,24},{1,5},{5... | collective-permute-start | bytes 12582920 | tf_op jit(solution)/shard_map/ppermute | solution.py:93
  530.5 14.9 %collective-permute-start.33 = (bf16[64,2048]{1,0:T(8,128)(2,1)S(1)}, bf16[64,2048]{1,0:T(8,128)(2,1)S(1)}, u32[]{:S(2)}, u32[]{:S(2)}) collective-permute-start(bf16[64,2048]{1,0:T(8,128)(2,1)S(1)} %get-tuple-element.105), channel_id=1, source_target_pairs={{0,8},{4,12},{8,0},{12,4},{16,24},{20,28},{24,16},{28,20},{1,9},{5... | collective-permute-start | bytes 786440 | tf_op jit(solution)/shard_map/ppermute | solution.py:93
  532.4 15.2 %collective-permute-start.36 = (bf16[64,2048]{1,0:T(8,128)(2,1)S(1)}, bf16[64,2048]{1,0:T(8,128)(2,1)S(1)}, u32[]{:S(2)}, u32[]{:S(2)}) collective-permute-start(bf16[64,2048]{1,0:T(8,128)(2,1)S(1)} %get-tuple-element.106), channel_id=1, source_target_pairs={{0,16},{4,20},{8,24},{12,28},{16,0},{20,4},{24,8},{28,12},{1,17},{... | collective-permute-start | bytes 786440 | tf_op jit(solution)/shard_map/ppermute | solution.py:93
  533.4 20.1 %collective-permute-start.34 = (bf16[64,2048]{1,0:T(8,128)(2,1)S(1)}, bf16[64,2048]{1,0:T(8,128)(2,1)S(1)}, u32[]{:S(2)}, u32[]{:S(2)}) collective-permute-start(bf16[64,2048]{1,0:T(8,128)(2,1)S(1)} %get-tuple-element.106), channel_id=1, source_target_pairs={{0,8},{4,12},{8,0},{12,4},{16,24},{20,28},{24,16},{28,20},{1,9},{5... | collective-permute-start | bytes 786440 | tf_op jit(solution)/shard_map/ppermute | solution.py:93
  534.9 18.7 %collective-permute-start.35 = (bf16[64,2048]{1,0:T(8,128)(2,1)S(1)}, bf16[64,2048]{1,0:T(8,128)(2,1)S(1)}, u32[]{:S(2)}, u32[]{:S(2)}) collective-permute-start(bf16[64,2048]{1,0:T(8,128)(2,1)S(1)} %get-tuple-element.105), channel_id=1, source_target_pairs={{0,16},{4,20},{8,24},{12,28},{16,0},{20,4},{24,8},{28,12},{1,17},{... | collective-permute-start | bytes 786440 | tf_op jit(solution)/shard_map/ppermute | solution.py:93
  618.6 23.1 %collective-permute-start.44 = (bf16[1024,128]{1,0:T(8,128)(2,1)}, bf16[1024,128]{1,0:T(8,128)(2,1)}, u32[]{:S(2)}, u32[]{:S(2)}) collective-permute-start(bf16[1024,128]{1,0:T(8,128)(2,1)} %bitcast.48), channel_id=1, source_target_pairs={{0,2},{1,3},{2,0},{3,1},{4,6},{5,7},{6,4},{7,5},{8,10},{9,11},{10,... | collective-permute-start | bytes 786440 | tf_op jit(solution)/shard_map/ppermute | solution.py:47
  618.6 23.1 %collective-permute-start.45 = (bf16[1024,128]{1,0:T(8,128)(2,1)}, bf16[1024,128]{1,0:T(8,128)(2,1)}, u32[]{:S(2)}, u32[]{:S(2)}) collective-permute-start(bf16[1024,128]{1,0:T(8,128)(2,1)} %bitcast.49), channel_id=1, source_target_pairs={{0,1},{1,2},{2,3},{3,0},{4,5},{5,6},{6,7},{7,4},{8,9},{9,10},{10,1... | collective-permute-start | bytes 786440 | tf_op jit(solution)/shard_map/ppermute | solution.py:47
  653.6 23.1 %collective-permute-start.46 = (bf16[4,128,2048]{2,1,0:T(8,128)(2,1)}, bf16[4,128,2048]{2,1,0:T(8,128)(2,1)}, u32[]{:S(2)}, u32[]{:S(2)}) collective-permute-start(bf16[4,128,2048]{2,1,0:T(8,128)(2,1)} %bitcast.51), channel_id=1, source_target_pairs={{0,4},{4,0},{8,12},{12,8},{16,20},{20,16},{24,28},{28,24},{1,5},{5... | collective-permute-start | bytes 6291464 | tf_op jit(solution)/shard_map/ppermute | solution.py:93
  663.0 119.0 %collective-permute-start.30 = (bf16[128,2048]{1,0:T(8,128)(2,1)}, bf16[128,2048]{1,0:T(8,128)(2,1)}, u32[]{:S(2)}, u32[]{:S(2)}) collective-permute-start(bf16[128,2048]{1,0:T(8,128)(2,1)} %get-tuple-element.68), channel_id=1, source_target_pairs={{0,3},{1,0},{2,1},{3,2},{4,7},{5,4},{6,5},{7,6},{8,11},{9,8},{10,9... | collective-permute-start | bytes 1572872 | tf_op jit(solution)/shard_map/ppermute | solution.py:47
  671.3 82.0 %all-to-all-start.2 = ((bf16[4,8,72,384]{3,2,1,0:T(8,128)(2,1)}), bf16[4,8,72,384]{3,2,1,0:T(8,128)(2,1)}, u32[]{:S(2)}, u32[]{:S(2)}) async-start(bf16[4,8,72,384]{3,2,1,0:T(8,128)(2,1)} %pad_maximum_fusion.5), calls=%async_computation.2 | async-start | bytes 3538944 | tf_op jit(solution)/shard_map/all_to_all | solution.py:52
  684.5 31.9 %collective-permute-start.51 = (bf16[64,2048]{1,0:T(8,128)(2,1)S(1)}, bf16[64,2048]{1,0:T(8,128)(2,1)S(1)}, u32[]{:S(2)}, u32[]{:S(2)}) collective-permute-start(bf16[64,2048]{1,0:T(8,128)(2,1)S(1)} %get-tuple-element.88), channel_id=1, source_target_pairs={{0,1},{1,2},{2,3},{3,0},{4,5},{5,6},{6,7},{7,4},{8,9},{9,10},{10,1... | collective-permute-start | bytes 786440 | tf_op jit(solution)/shard_map/ppermute | solution.py:59
  686.6 60.7 %collective-permute-start.52 = (bf16[64,2048]{1,0:T(8,128)(2,1)S(1)}, bf16[64,2048]{1,0:T(8,128)(2,1)S(1)}, u32[]{:S(2)}, u32[]{:S(2)}) collective-permute-start(bf16[64,2048]{1,0:T(8,128)(2,1)S(1)} %get-tuple-element.90), channel_id=1, source_target_pairs={{0,2},{1,3},{2,0},{3,1},{4,6},{5,7},{6,4},{7,5},{8,10},{9,11},{10,... | collective-permute-start | bytes 786440 | tf_op jit(solution)/shard_map/ppermute | solution.py:59
  689.0 62.7 %collective-permute-start.53 = (bf16[64,2048]{1,0:T(8,128)(2,1)S(1)}, bf16[64,2048]{1,0:T(8,128)(2,1)S(1)}, u32[]{:S(2)}, u32[]{:S(2)}) collective-permute-start(bf16[64,2048]{1,0:T(8,128)(2,1)S(1)} %get-tuple-element.89), channel_id=1, source_target_pairs={{0,3},{1,0},{2,1},{3,2},{4,7},{5,4},{6,5},{7,6},{8,11},{9,8},{10,9... | collective-permute-start | bytes 786440 | tf_op jit(solution)/shard_map/ppermute | solution.py:59
  693.7 66.6 %collective-permute-start.49 = (bf16[2,64,2048]{2,1,0:T(8,128)(2,1)}, bf16[2,64,2048]{2,1,0:T(8,128)(2,1)}, u32[]{:S(2)}, u32[]{:S(2)}) collective-permute-start(bf16[2,64,2048]{2,1,0:T(8,128)(2,1)} %stack.70), channel_id=1, source_target_pairs={{0,16},{4,20},{8,24},{12,28},{16,0},{20,4},{24,8},{28,12},{1,17},{... | collective-permute-start | bytes 1572872 | tf_op jit(solution)/shard_map/ppermute | solution.py:93
  716.4 65.6 %collective-permute-start.31 = (bf16[128,2048]{1,0:T(8,128)(2,1)}, bf16[128,2048]{1,0:T(8,128)(2,1)}, u32[]{:S(2)}, u32[]{:S(2)}) collective-permute-start(bf16[128,2048]{1,0:T(8,128)(2,1)} %get-tuple-element.70), channel_id=1, source_target_pairs={{0,2},{1,3},{2,0},{3,1},{4,6},{5,7},{6,4},{7,5},{8,10},{9,11},{10,... | collective-permute-start | bytes 1572872 | tf_op jit(solution)/shard_map/ppermute | solution.py:47
  747.3 34.7 %collective-permute-start.32 = (bf16[128,2048]{1,0:T(8,128)(2,1)}, bf16[128,2048]{1,0:T(8,128)(2,1)}, u32[]{:S(2)}, u32[]{:S(2)}) collective-permute-start(bf16[128,2048]{1,0:T(8,128)(2,1)} %get-tuple-element.69), channel_id=1, source_target_pairs={{0,1},{1,2},{2,3},{3,0},{4,5},{5,6},{6,7},{7,4},{8,9},{9,10},{10,1... | collective-permute-start | bytes 1572872 | tf_op jit(solution)/shard_map/ppermute | solution.py:47
  780.1 17.4 %collective-permute-start.57 = (bf16[64,2048]{1,0:T(8,128)(2,1)}, bf16[64,2048]{1,0:T(8,128)(2,1)}, u32[]{:S(2)}, u32[]{:S(2)}) collective-permute-start(bf16[64,2048]{1,0:T(8,128)(2,1)} %get-tuple-element.82), channel_id=1, source_target_pairs={{0,1},{1,2},{2,3},{3,0},{4,5},{5,6},{6,7},{7,4},{8,9},{9,10},{10,1... | collective-permute-start | bytes 786440 | tf_op jit(solution)/shard_map/ppermute | solution.py:70
  785.9 30.1 %collective-permute-start.58 = (bf16[64,2048]{1,0:T(8,128)(2,1)}, bf16[64,2048]{1,0:T(8,128)(2,1)}, u32[]{:S(2)}, u32[]{:S(2)}) collective-permute-start(bf16[64,2048]{1,0:T(8,128)(2,1)} %get-tuple-element.81), channel_id=1, source_target_pairs={{0,2},{1,3},{2,0},{3,1},{4,6},{5,7},{6,4},{7,5},{8,10},{9,11},{10,... | collective-permute-start | bytes 786440 | tf_op jit(solution)/shard_map/ppermute | solution.py:70
  787.4 30.3 %collective-permute-start.59 = (bf16[64,2048]{1,0:T(8,128)(2,1)S(1)}, bf16[64,2048]{1,0:T(8,128)(2,1)S(1)}, u32[]{:S(2)}, u32[]{:S(2)}) collective-permute-start(bf16[64,2048]{1,0:T(8,128)(2,1)S(1)} %get-tuple-element.80), channel_id=1, source_target_pairs={{0,3},{1,0},{2,1},{3,2},{4,7},{5,4},{6,5},{7,6},{8,11},{9,8},{10,9... | collective-permute-start | bytes 786440 | tf_op jit(solution)/shard_map/ppermute | solution.py:70
  791.7 28.2 %collective-permute-start.54 = (bf16[64,2048]{1,0:T(8,128)(2,1)S(1)}, bf16[64,2048]{1,0:T(8,128)(2,1)}, u32[]{:S(2)}, u32[]{:S(2)}) collective-permute-start(bf16[64,2048]{1,0:T(8,128)(2,1)S(1)} %get-tuple-element.86), channel_id=1, source_target_pairs={{0,1},{1,2},{2,3},{3,0},{4,5},{5,6},{6,7},{7,4},{8,9},{9,10},{10,1... | collective-permute-start | bytes 786440 | tf_op jit(solution)/shard_map/ppermute | solution.py:70
  791.8 43.2 %collective-permute-start.55 = (bf16[64,2048]{1,0:T(8,128)(2,1)S(1)}, bf16[64,2048]{1,0:T(8,128)(2,1)}, u32[]{:S(2)}, u32[]{:S(2)}) collective-permute-start(bf16[64,2048]{1,0:T(8,128)(2,1)S(1)} %get-tuple-element.85), channel_id=1, source_target_pairs={{0,2},{1,3},{2,0},{3,1},{4,6},{5,7},{6,4},{7,5},{8,10},{9,11},{10,... | collective-permute-start | bytes 786440 | tf_op jit(solution)/shard_map/ppermute | solution.py:70
  792.4 53.8 %all-to-all-start.4 = ((bf16[4,64,2048]{2,1,0:T(8,128)(2,1)}), bf16[4,64,2048]{2,1,0:T(8,128)(2,1)S(1)}, u32[]{:S(2)}, u32[]{:S(2)}) async-start(bf16[4,64,2048]{2,1,0:T(8,128)(2,1)} %bitcast.210), calls=%async_computation.7 | async-start | bytes 2097152 | tf_op jit(solution)/shard_map/all_to_all | solution.py:52
  797.4 38.5 %collective-permute-start.56 = (bf16[64,2048]{1,0:T(8,128)(2,1)S(1)}, bf16[64,2048]{1,0:T(8,128)(2,1)S(1)}, u32[]{:S(2)}, u32[]{:S(2)}) collective-permute-start(bf16[64,2048]{1,0:T(8,128)(2,1)S(1)} %get-tuple-element.84), channel_id=1, source_target_pairs={{0,3},{1,0},{2,1},{3,2},{4,7},{5,4},{6,5},{7,6},{8,11},{9,8},{10,9... | collective-permute-start | bytes 786440 | tf_op jit(solution)/shard_map/ppermute | solution.py:70
  (50 other events, 530.7 us)
Sparse Core Ops, SparseCore 0:
  25.3 55.3 all-gather.4
  83.1 54.1 all-gather.6
  203.3 53.1 all-gather.8
  258.2 58.5 all-gather.10
  443.4 64.5 reduce-scatter.5
  510.8 69.4 reduce-scatter.3
  621.0 51.6 reduce-scatter.7
